TPU v7x, 128 devices: a whole 4x4x4 slice. The times are simulated.
128 devices in a mesh: lon: 32 (over y, x_hi, z), band: 4 (over x_lo, core).
Axes of the slice: x: 4 (x_hi: 2, x_lo: 2; x = x_hi * 2 + x_lo), y: 4, z: 4, core: 2. Of those that a mesh axis runs over, the one named last changes fastest.
Arguments:
- denoised_tokens: bfloat16 [4, 32, 7680], P('band', 'lon'), may hold values from -6 to 6
- sequence_row_index: int32 [4, 32], P('band'), may hold values from 0 to 31, each once within a row
- latent_frame_cache: bfloat16 [4, 128, 7680], P(None, 'band', 'lon'), may hold values from -6 to 6
- cache_slot_order: int32 [4], replicated, may hold values from 0 to 3, each once
- temporal_taps_weight: bfloat16 [3, 16, 16], replicated, may hold values from -0.875 to 0.875
- input_weight: bfloat16 [9, 16, 256], replicated, may hold values from -0.5 to 0.5
- latent_conv_weights: bfloat16 [2, 9, 256, 256], replicated, may hold values from -0.125 to 0.125
- upsampled_weight: bfloat16 [9, 256, 256], replicated, may hold values from -0.125 to 0.125
- upper_conv_weights: bfloat16 [2, 9, 256, 256], replicated, may hold values from -0.125 to 0.125
- latent_norm_gains: float32 [2, 256], replicated, may hold values from 0.5 to 1.5
- upper_norm_gains: float32 [2, 256], replicated, may hold values from 0.5 to 1.5
Outputs:
- decoded: bfloat16 [256, 960, 256], P('band', 'lon')
Inputs may be any that keep to these rules, and one draw needn't show every extreme that they name: Each row sequence_row_index[b] holds every position 0..31 once. cache_slot_order holds each slot once.
All inputs are finite; a program needn't handle non-finite values.
Results may differ from a plain program's by a relative error of at most 0.02.
Values may be sent and summed in bfloat16 or wider, within the bound.
No kernel may reach another device: no remote copies, remote signals or barrier semaphores. Data moves between devices by JAX's collectives and lax.ppermute only.
A program may use at most 128 MiB of HBM per device.

v0:
```python
import functools

import jax
import jax.numpy as jnp
from jax import lax
from jax.experimental import pallas as pl
from jax.experimental.pallas import tpu as pltpu
from jax.sharding import PartitionSpec as P

F32 = jnp.float32
BF16 = jnp.bfloat16

N_LON = 32
N_BAND = 4
N_DEV = N_LON * N_BAND
ROWS = 32
COLS = 15
LAT = 16
CH = 256
HALO = 5
TOKEN = 480 * LAT
LANES = COLS * LAT
EDGE = HALO * LAT
WINDOW = LANES + 2 * EDGE
CHUNK = 24


def window_start(lon):
    return (LANES * lon - EDGE) // 128


def window_offset(lon):
    return (LANES * lon - EDGE) % 128


def iota(shape, dim):
    return lax.broadcasted_iota(jnp.int32, shape, dim)


def block_diagonal(tap):
    rows = jnp.where(iota((128, LAT), 0) % LAT == iota((128, LAT), 1), 1.0, 0.0).astype(BF16)
    cols = jnp.where(iota((LAT, 128), 1) % LAT == iota((LAT, 128), 0), 1.0, 0.0).astype(BF16)
    tall = jnp.dot(rows, tap, preferred_element_type=F32).astype(BF16)
    full = jnp.dot(tall, cols, preferred_element_type=F32)
    same = iota((128, 128), 0) // LAT == iota((128, 128), 1) // LAT
    return jnp.where(same, full, 0.0).astype(BF16)


def pack_kernel(index_ref, slot_ref, token_ref, cache_ref, taps_ref, send_ref, own_ref, x_ref):
    lon = lax.axis_index("lon")
    band = lax.axis_index("band")
    row = jnp.int32(0)
    for r in range(ROWS):
        row = jnp.where(index_ref[0, r] == lon, r, row)
    tag = row.astype(F32)
    for k in range(TOKEN // 128):
        piece = token_ref[0, :, 128 * k : 128 * k + 128].astype(F32)
        x_ref[k : k + 1, :] = piece
        if k < 4:
            x_ref[60 + k : 61 + k, :] = piece
    place = iota((8, 128), 0) * 128 + iota((8, 128), 1)
    for target in range(N_LON):
        start = window_start(target) % 60
        spot = (window_offset(target) + WINDOW) % 512
        tile = x_ref[start : start + 8, :]
        tile = jnp.where(place == spot, tag, tile).astype(BF16)
        for b in range(N_BAND):
            send_ref[target * N_BAND + b, 0:8, :] = tile

    diagonals = [block_diagonal(taps_ref[t]) for t in (1, 2)]
    mixed = jnp.zeros((2 * ROWS, 128), F32)
    for t in range(2):
        frame = cache_ref[slot_ref[t]]
        frame = jnp.concatenate([frame, jnp.zeros((ROWS, 256 - LANES), BF16)], axis=1)
        stacked = jnp.concatenate([frame[:, :128], frame[:, 128:]], axis=0)
        mixed = mixed + jnp.dot(stacked, diagonals[t], preferred_element_type=F32)
    own = jnp.concatenate([mixed[:ROWS], mixed[ROWS:]], axis=1)
    own_ref[...] = own

    def send(d_lon, d_band, part):
        rest = CHUNK - 4 - part.shape[0]
        full = [jnp.zeros((4, 128), F32), part]
        if rest:
            full.append(jnp.zeros((rest, 128), F32))
        full = jnp.concatenate(full, axis=0)
        to = lax.rem(lon + d_lon + N_LON, N_LON) * N_BAND + lax.rem(band + d_band + N_BAND, N_BAND)
        first = send_ref[to, 0:8, :].astype(F32)
        send_ref[to, 0:8, :] = jnp.where(iota((8, 128), 0) < 4, first, full[:8]).astype(BF16)
        send_ref[to, 8:CHUNK, :] = full[8:].astype(BF16)

    def tall(v):
        top = jnp.concatenate([v[:16, :EDGE], v[16:, : 128 - EDGE]], axis=1)
        low = jnp.concatenate(
            [v[16 + 4 * m : 20 + 4 * m, 128 - EDGE : EDGE] for m in range(4)], axis=1
        )
        return jnp.concatenate([top, low], axis=0)

    def corner(v):
        return jnp.concatenate([v, jnp.zeros((HALO, 128 - EDGE), F32)], axis=1)

    left, right = own[:, :EDGE], own[:, LANES - EDGE : LANES]
    send(-1, 0, tall(left))
    send(1, 0, tall(right))
    for d_band, rows in ((-1, slice(0, HALO)), (1, slice(ROWS - HALO, ROWS))):
        wide = own[rows]
        send(0, d_band, jnp.concatenate([wide[:, :128], wide[:, 128:]], axis=0))
        send(-1, d_band, corner(left[rows]))
        send(1, d_band, corner(right[rows]))


def activate(values, gain):
    mean = jnp.sum(values * values, axis=-1, keepdims=True) * (1.0 / CH)
    half = values * lax.rsqrt(mean + 1e-06) * (0.5 * gain)
    return half * jnp.tanh(half) + half


def roll_rows(values, by):
    return pltpu.roll(values, by % values.shape[0], axis=0)


LOW = 32
HIGH = 16


def block_kernel(
    got_ref,
    own_ref,
    taps_ref,
    low_gain_ref,
    high_gain_ref,
    w_in_hbm,
    w_low_hbm,
    w_up_hbm,
    w_high_hbm,
    out_hbm,
    w_in,
    w_low,
    w_up,
    w_high,
    w_phase,
    tok_ref,
    u_ref,
    open_ref,
    a1_ref,
    a2_ref,
    low_ref,
    s1_ref,
    raw_ref,
    s2_ref,
    mix_ref,
    out_ref,
    in_sem,
    out_sem,
):
    lon = lax.axis_index("lon")
    band = lax.axis_index("band")
    copies = [pltpu.make_async_copy(w_in_hbm.at[p], w_in.at[p, 0:48], in_sem.at[p]) for p in range(3)]
    copies.append(pltpu.make_async_copy(w_low_hbm.at[0], w_low.at[0], in_sem.at[3]))
    copies.append(pltpu.make_async_copy(w_low_hbm.at[1], w_low.at[1], in_sem.at[4]))
    copies.append(pltpu.make_async_copy(w_up_hbm, w_up, in_sem.at[5]))
    copies.append(pltpu.make_async_copy(w_high_hbm.at[0], w_high.at[0], in_sem.at[6]))
    copies.append(pltpu.make_async_copy(w_high_hbm.at[1], w_high.at[1], in_sem.at[7]))
    w_in[:, 48:128, :] = jnp.zeros((3, 80, CH), BF16)
    for copy in copies:
        copy.start()

    tok_ref[...] = got_ref[:, 0:8, :].astype(F32).reshape(N_DEV * 8, 128)
    x = jnp.concatenate([tok_ref[pl.ds(k, N_DEV, stride=8), :] for k in range(4)], axis=1)
    offset = lax.rem(LANES * lon + (128 - EDGE), 128)
    x = pltpu.roll(x, lax.rem(512 - offset, 512), axis=1)
    tag = x[:, WINDOW : WINDOW + 1].astype(jnp.int32)
    m = iota((N_DEV, 128), 1)
    want_band = jnp.where(m < HALO, band - 1, jnp.where(m < HALO + ROWS, band, band + 1))
    want_row = jnp.where(
        m < HALO, m + ROWS - HALO, jnp.where(m < HALO + ROWS, m - HALO, m - HALO - ROWS)
    )
    want_row = jnp.where(m < 2 * HALO + ROWS, want_row, -1)
    hit = (tag == want_row) & (iota((N_DEV, 128), 0) % N_BAND == want_band)
    select = jnp.where(hit, 1.0, 0.0).T[:48].astype(BF16)
    latent = jnp.dot(select, x.astype(BF16), preferred_element_type=F32).astype(BF16)

    def chunk(d_lon, d_band):
        source = lax.rem(lon + d_lon + N_LON, N_LON) * N_BAND + lax.rem(band + d_band + N_BAND, N_BAND)
        return got_ref[source].astype(F32)[4:]

    def side(d_lon):
        c = chunk(d_lon, 0)
        low = jnp.concatenate([c[16:20, 32 * k : 32 * k + 32] for k in range(4)], axis=0)
        low = jnp.concatenate([c[:16, EDGE:], low], axis=1)
        return jnp.concatenate([c[:16, :EDGE], low], axis=0)

    def rim(d_band):
        c = chunk(0, d_band)
        parts = [
            chunk(-1, d_band)[:HALO, :EDGE],
            c[:HALO],
            c[HALO : 2 * HALO, : LANES - 128],
            chunk(1, d_band)[:HALO, :EDGE],
            jnp.zeros((HALO, 512 - WINDOW), F32),
        ]
        whole = jnp.concatenate(parts, axis=1)
        inside = (band + d_band >= 0) & (band + d_band < N_BAND)
        return jnp.where(inside, whole, 0.0)

    middle = jnp.concatenate(
        [side(-1), own_ref[:, :LANES], side(1), jnp.zeros((ROWS, 512 - WINDOW), F32)], axis=1
    )
    cached = jnp.concatenate([rim(-1), middle, rim(1), jnp.zeros((6, 512), F32)], axis=0)
    diagonal = block_diagonal(taps_ref[0])
    stacked = jnp.concatenate([latent[:, 128 * k : 128 * k + 128] for k in range(4)], axis=0)
    fresh = jnp.dot(stacked, diagonal, preferred_element_type=F32)
    fresh = jnp.concatenate([fresh[48 * k : 48 * k + 48] for k in range(4)], axis=1)
    temporal = (fresh + cached).astype(BF16).astype(F32)
    temporal = jnp.where(iota((48, 512), 1) < WINDOW, temporal, 0.0)

    wide = jnp.concatenate([temporal, jnp.zeros((48, 128), F32)], axis=1)
    for j in range(24):
        piece = wide[:, 128 * (j // 8) : 128 * (j // 8) + 256]
        turn = LAT * (j % 8)
        if turn:
            piece = pltpu.roll(piece, 256 - turn, axis=1)
        u_ref[j] = piece[:, :128]
    lhs = jnp.concatenate(
        [u_ref[:, p : p + 40, :].reshape(960, 128).astype(BF16) for p in range(3)], axis=1
    )
    for copy in copies[:3]:
        copy.wait()
    opening = jnp.dot(lhs, w_in[...].reshape(384, CH), preferred_element_type=F32)
    opening = opening.astype(BF16).astype(F32)
    for j in range(23):
        for half in range(2):
            open_ref[half, pl.ds(j, 40, stride=LOW), :] = opening[
                40 * j : 40 * j + 40, 128 * half : 128 * half + 128
            ]

    def opened(rows):
        return jnp.concatenate([open_ref[0, rows, :], open_ref[1, rows, :]], axis=1)

    def zero_rows(ref, pitch, top, bottom):
        total = ref.shape[0] // pitch

        @pl.when(band == 0)
        def _():
            ref[0 : top * pitch, :] = jnp.zeros((top * pitch, ref.shape[1]), ref.dtype)

        @pl.when(band == N_BAND - 1)
        def _():
            ref[(total - bottom) * pitch :, :] = jnp.zeros((bottom * pitch, ref.shape[1]), ref.dtype)

    def conv(ref, pitch, row, count, lane, weight):
        total = None
        for p in range(3):
            part = jnp.dot(
                ref[(row + p) * pitch : (row + p + count) * pitch, lane : lane + 3 * CH],
                weight[p],
                preferred_element_type=F32,
            )
            total = part if total is None else total + part
        return total

    def spread(act, ref, at):
        rows = slice(at, at + act.shape[0])
        ref[rows, 0:CH] = roll_rows(act, 1).astype(BF16)
        ref[rows, CH : 2 * CH] = act.astype(BF16)
        ref[rows, 2 * CH :] = roll_rows(act, -1).astype(BF16)

    gain = low_gain_ref[0:1, :]
    for r in range(0, 40, 10):
        rows = slice(r * LOW, (r + 10) * LOW)
        spread(activate(opened(rows), gain), a1_ref, r * LOW)
    zero_rows(a1_ref, LOW, 4, 4)
    copies[3].wait()
    gain = low_gain_ref[1:2, :]
    for r in range(0, 38, 19):
        inner = conv(a1_ref, LOW, r, 19, 0, w_low.at[0])
        spread(activate(inner, gain), a2_ref, r * LOW)
    zero_rows(a2_ref, LOW, 3, 3)
    copies[4].wait()
    for r in range(0, 36, 18):
        branch = conv(a2_ref, LOW, r, 18, 0, w_low.at[1])
        low = opened(slice((r + 2) * LOW, (r + 20) * LOW)) + branch
        for k in range(4):
            part = roll_rows(low, -(2 + k)).reshape(18, LOW, CH)[:, :HIGH]
            low_ref[r * HIGH : (r + 18) * HIGH, CH * k : CH * k + CH] = part.reshape(
                18 * HIGH, CH
            ).astype(BF16)
    zero_rows(low_ref, HIGH, 2, 2)

    copies[5].wait()
    for a in range(2):
        for r in range(2):
            taps = ((0,), (1, 2)) if a == 0 else ((0, 1), (2,))
            for odd in range(2):
                sides = ((0, 1), (2,)) if odd else ((0,), (1, 2))
                for c in range(2):
                    total = None
                    for p in taps[r]:
                        for q in sides[c]:
                            one = w_up[3 * p + q].astype(F32)
                            total = one if total is None else total + one
                    w_phase[a, r, CH * c : CH * c + CH, (1 - odd) * CH : (2 - odd) * CH] = (
                        total.astype(BF16)
                    )
    gain = high_gain_ref[0:1, :]
    for a in range(2):
        for n in range(0, 34, 17):

            def phase(lane, out_lane, width):
                total = None
                for r in range(2):
                    at = (n + a + r) * HIGH
                    part = jnp.dot(
                        low_ref[at : at + 17 * HIGH, lane : lane + 2 * CH],
                        w_phase[a, r, :, out_lane : out_lane + width],
                        preferred_element_type=F32,
                    )
                    total = part if total is None else total + part
                return total.astype(BF16).astype(F32)

            def put(value, slot, raw_slot):
                act = activate(value, gain).astype(BF16)
                raw = value.astype(BF16)
                for i in range(17):
                    at = (2 * (n + i) + a) * HIGH
                    rows = slice(i * HIGH, (i + 1) * HIGH)
                    s1_ref[at : at + HIGH, CH * slot : CH * slot + CH] = act[rows]
                    if raw_slot is not None:
                        raw_ref[at : at + HIGH, CH * raw_slot : CH * raw_slot + CH] = raw[rows]

            both = phase(CH, 0, 2 * CH)
            put(both[:, :CH], 1, None)
            put(both[:, CH:], 2, 0)
            put(phase(2 * CH, 0, CH), 3, 1)
            put(phase(0, CH, CH), 0, None)
    zero_rows(s1_ref, HIGH, 2, 2)

    copies[6].wait()
    gain = high_gain_ref[1:2, :]
    for r in range(0, 66, 22):
        rows = slice(r * HIGH, (r + 22) * HIGH)
        odd = activate(conv(s1_ref, HIGH, r, 22, 0, w_high.at[0]), gain)
        s2_ref[rows, 0:CH] = odd.astype(BF16)
        s2_ref[rows, 2 * CH : 3 * CH] = roll_rows(odd, -1).astype(BF16)
        even = activate(conv(s1_ref, HIGH, r, 22, CH, w_high.at[0]), gain)
        s2_ref[rows, CH : 2 * CH] = even.astype(BF16)
        s2_ref[rows, 3 * CH :] = roll_rows(even, -1).astype(BF16)
    zero_rows(s2_ref, HIGH, 1, 1)
    copies[7].wait()
    outs = []
    for n, r in enumerate(range(0, 64, 16)):
        rows = slice((r + 2) * HIGH, (r + 18) * HIGH)
        even = conv(s2_ref, HIGH, r, 16, 0, w_high.at[1]) + raw_ref[rows, :CH].astype(F32)
        odd = conv(s2_ref, HIGH, r, 16, CH, w_high.at[1]) + raw_ref[rows, CH:].astype(F32)
        for half in range(2):
            lanes = slice(128 * half, 128 * half + 128)
            mix_ref[n % 2, half, pl.ds(0, 16 * HIGH, stride=2), :] = even[:, lanes]
            mix_ref[n % 2, half, pl.ds(1, 16 * HIGH, stride=2), :] = odd[:, lanes]
            out_ref[r : r + 16, :, lanes] = (
                mix_ref[n % 2, half].astype(BF16).reshape(16, 32, 128)[:, :30]
            )
        copy = pltpu.make_async_copy(
            out_ref.at[r : r + 16], out_hbm.at[r : r + 16], out_sem.at[n]
        )
        copy.start()
        outs.append(copy)
    for copy in outs:
        copy.wait()


def shards(
    denoised_tokens,
    sequence_row_index,
    latent_frame_cache,
    cache_slot_order,
    temporal_taps_weight,
    input_weight,
    latent_conv_weights,
    upsampled_weight,
    upper_conv_weights,
    latent_norm_gains,
    upper_norm_gains,
):
    struct = jax.ShapeDtypeStruct
    vmem = pl.BlockSpec(memory_space=pltpu.VMEM)
    smem = pl.BlockSpec(memory_space=pltpu.SMEM)
    anywhere = pl.BlockSpec(memory_space=pl.ANY)
    payload, own = pl.pallas_call(
        pack_kernel,
        in_specs=[smem, smem, vmem, vmem, vmem],
        out_specs=[vmem, vmem],
        out_shape=[struct((N_DEV, CHUNK, 128), BF16), struct((ROWS, 256), F32)],
        scratch_shapes=[pltpu.VMEM((72, 128), F32)],
        name="pack",
    )(
        sequence_row_index,
        cache_slot_order,
        denoised_tokens,
        latent_frame_cache,
        temporal_taps_weight,
    )
    arrived = lax.all_to_all(payload, ("lon", "band"), 0, 0, tiled=True)
    return pl.pallas_call(
        block_kernel,
        in_specs=[vmem] * 5 + [anywhere] * 4,
        out_specs=anywhere,
        out_shape=struct((2 * ROWS, 2 * COLS, CH), BF16),
        scratch_shapes=[
            pltpu.VMEM((3, 128, CH), BF16),
            pltpu.VMEM((2, 3, 3 * CH, CH), BF16),
            pltpu.VMEM((9, CH, CH), BF16),
            pltpu.VMEM((2, 3, 3 * CH, CH), BF16),
            pltpu.VMEM((2, 2, 2 * CH, 2 * CH), BF16),
            pltpu.VMEM((N_DEV * 8, 128), F32),
            pltpu.VMEM((24, 48, 128), F32),
            pltpu.VMEM((2, 40 * LOW, 128), F32),
            pltpu.VMEM((40 * LOW, 3 * CH), BF16),
            pltpu.VMEM((38 * LOW, 3 * CH), BF16),
            pltpu.VMEM((36 * HIGH, 4 * CH), BF16),
            pltpu.VMEM((68 * HIGH, 4 * CH), BF16),
            pltpu.VMEM((68 * HIGH, 2 * CH), BF16),
            pltpu.VMEM((66 * HIGH, 4 * CH), BF16),
            pltpu.VMEM((2, 2, 2 * 16 * HIGH, 128), F32),
            pltpu.VMEM((2 * ROWS, 2 * COLS, CH), BF16),
            pltpu.SemaphoreType.DMA((8,)),
            pltpu.SemaphoreType.DMA((4,)),
        ],
        compiler_params=pltpu.CompilerParams(vmem_limit_bytes=50 * 1024 * 1024),
        name="block",
    )(
        arrived,
        own,
        temporal_taps_weight,
        latent_norm_gains,
        upper_norm_gains,
        input_weight.reshape(3, 48, CH),
        latent_conv_weights.reshape(2, 3, 3 * CH, CH),
        upsampled_weight,
        upper_conv_weights.reshape(2, 3, 3 * CH, CH),
    )


def solution(mesh):
    in_specs = (
        P("band", "lon", None),
        P("band", None),
        P(None, "band", "lon"),
        P(),
        P(),
        P(),
        P(),
        P(),
        P(),
        P(),
        P(),
    )
    out_specs = P("band", "lon", None)
    return jax.shard_map(shards, mesh=mesh, in_specs=in_specs, out_specs=out_specs, check_vma=False)
```

profile of v0, /device:TPU:1, one launch (start us, length us, event | category | flops | bytes accessed | tf_op | source)
XLA Modules:
  0.0 52.8 jit_solution(9352613951244657205)
XLA Ops:
  0.0 0.0 copy-start
  0.0 2.3 %pack.1 = (bf16[128,24,128]{2,1,0:T(8,128)(2,1)}, f32[32,256]{1,0:T(8,128)}) custom-call(s32[1,32]{1,0:T(1,128)} %index_ref.1, s32[4]{0:T(128)} %slot_ref.1, bf16[1,1,7680]{2,1,0:T(2,128)(2,1)} %token_ref.1, bf16[4,32,240]{2,1,0:T(8,128)(2,1)} %cache_ref.1, bf16[3,16,16]{2,1,0:T(8,128)(2,1)} %taps_ref.3), custom_call_target="tpu_custom_call" | custom-call | tf_op jit(solution)/shard_map/pack/pallas_call | solution.py:387
  2.3 28.1 %all_to_all.5.got_ref = bf16[128,24,128]{2,1,0:T(8,128)(2,1)S(1)} all-to-all(bf16[128,24,128]{2,1,0:T(8,128)(2,1)} %get-tuple-element.7), channel_id=1, replica_groups=mesh['lon'=32,'band'=4] {'lon','band'}, dimensions={0} | all-to-all | bytes 1572864 | tf_op jit(solution)/shard_map/all_to_all | solution.py:401
  30.5 0.0 copy-done
  30.5 0.0 copy-start.1
  30.5 0.9 %copy-done.1 = bf16[9,16,256]{2,1,0:T(8,128)(2,1)S(1)} copy-done((bf16[9,16,256]{2,1,0:T(8,128)(2,1)S(1)}, bf16[9,16,256]{2,1,0:T(8,128)(2,1)}, u32[]{:S(2)}) %copy-start.1) | copy-done | bytes 73752
  31.4 0.0 copy-start.2
  31.4 0.7 %copy-done.2 = bf16[3,16,16]{2,1,0:T(8,128)(2,1)S(1)} copy-done((bf16[3,16,16]{2,1,0:T(8,128)(2,1)S(1)}, bf16[3,16,16]{2,1,0:T(8,128)(2,1)}, u32[]{:S(2)}) %copy-start.2) | copy-done | bytes 1560
  32.1 0.0 copy-start.3
  32.1 0.8 %copy-done.3 = f32[32,256]{1,0:T(8,128)S(1)} copy-done((f32[32,256]{1,0:T(8,128)S(1)}, f32[32,256]{1,0:T(8,128)}, u32[]{:S(2)}) %copy-start.3) | copy-done | bytes 32792
  32.8 0.0 copy-start.4
  32.8 0.7 %copy-done.4 = f32[2,256]{1,0:T(2,128)S(1)} copy-done((f32[2,256]{1,0:T(2,128)S(1)}, f32[2,256]{1,0:T(2,128)}, u32[]{:S(2)}) %copy-start.4) | copy-done | bytes 2072
  33.5 0.0 copy-start.5
  33.5 0.7 %copy-done.5 = f32[2,256]{1,0:T(2,128)S(1)} copy-done((f32[2,256]{1,0:T(2,128)S(1)}, f32[2,256]{1,0:T(2,128)}, u32[]{:S(2)}) %copy-start.5) | copy-done | bytes 2072
  34.2 17.1 %block.1 = bf16[64,30,256]{2,1,0:T(8,128)(2,1)S(1)} custom-call(bf16[128,24,128]{2,1,0:T(8,128)(2,1)S(1)} %all_to_all.5.got_ref, f32[32,256]{1,0:T(8,128)S(1)} %copy-done.3, bf16[3,16,16]{2,1,0:T(8,128)(2,1)S(1)} %copy-done.2, f32[2,256]{1,0:T(2,128)S(1)} %copy-done.4, f32[2,256]{1,0:T(2,128)S(1)} %copy-done.5, bf16[3,48,256]{2,1,0:T(8,128)(2,1)S(1)} %bitcast.3, ...), custom_call_target="tpu_custom_call" | custom-call | tf_op jit(solution)/shard_map/block/pallas_call | solution.py:402
  51.3 1.5 %copy.12 = bf16[64,30,256]{2,0,1:T(8,128)(2,1)} copy(bf16[64,30,256]{2,1,0:T(8,128)(2,1)S(1)} %block.1) | data formatting | bytes 1966080 | tf_op jit(solution)/shard_map/block/pallas_call | solution.py:402
Async XLA Ops:
  0.0 30.5 %copy-start = (bf16[9,256,256]{2,1,0:T(8,128)(2,1)S(1)}, bf16[9,256,256]{2,1,0:T(8,128)(2,1)}, u32[]{:S(2)}) copy-start(bf16[9,256,256]{2,1,0:T(8,128)(2,1)} %w_up_hbm.1) | copy-start | bytes 3538948
  30.5 0.9 %copy-start.1 = (bf16[9,16,256]{2,1,0:T(8,128)(2,1)S(1)}, bf16[9,16,256]{2,1,0:T(8,128)(2,1)}, u32[]{:S(2)}) copy-start(bf16[9,16,256]{2,1,0:T(8,128)(2,1)} %param.16) | copy-start | bytes 221188
  31.4 0.7 %copy-start.2 = (bf16[3,16,16]{2,1,0:T(8,128)(2,1)S(1)}, bf16[3,16,16]{2,1,0:T(8,128)(2,1)}, u32[]{:S(2)}) copy-start(bf16[3,16,16]{2,1,0:T(8,128)(2,1)} %taps_ref.3) | copy-start | bytes 4612
  32.1 0.8 %copy-start.3 = (f32[32,256]{1,0:T(8,128)S(1)}, f32[32,256]{1,0:T(8,128)}, u32[]{:S(2)}) copy-start(f32[32,256]{1,0:T(8,128)} %get-tuple-element.8.own_ref) | copy-start | bytes 98308
  32.8 0.7 %copy-start.4 = (f32[2,256]{1,0:T(2,128)S(1)}, f32[2,256]{1,0:T(2,128)}, u32[]{:S(2)}) copy-start(f32[2,256]{1,0:T(2,128)} %low_gain_ref.1) | copy-start | bytes 6148
  33.5 0.7 %copy-start.5 = (f32[2,256]{1,0:T(2,128)S(1)}, f32[2,256]{1,0:T(2,128)}, u32[]{:S(2)}) copy-start(f32[2,256]{1,0:T(2,128)} %high_gain_ref.1) | copy-start | bytes 6148
where the time goes:
time: 53.2 us; the launch traced here: 52.8 us
  blocking collectives  28.1 us (53%)
  Pallas kernels  19.5 us (37%)
  local copies, waits for them, and re-layouts  5.21 us (10%)
    all_to_all x1, blocking collectives, shards(): arrived = lax.all_to_all(payload, ('lon', 'band'), 0, 0, tiled=True)  28.1 us
    pallas_call x1, Pallas kernels, shards(): pl.pallas_call(block_kernel, in_specs=[vmem] * 5 + [anywhere] * 4, out_sp...  17.1 us
    unnamed x12, local copies, waits for them, and re-layouts  3.71 us
    pallas_call x1, Pallas kernels, shards(): pl.pallas_call(pack_kernel, in_specs=[smem, smem, vmem, vmem, vmem], out_...  2.33 us
    pallas_call x1, local copies, waits for them, and re-layouts, shards(): pl.pallas_call(block_kernel, in_specs=[vmem] * 5 + [anywhere] * 4, out_sp...  1.49 us

commit v1 on v0

--- a/solution.py
+++ b/solution.py
@@ -118,21 +118,32 @@
     return pltpu.roll(values, by % values.shape[0], axis=0)
 
 
-LOW = 32
+def cuts(rows, pieces):
+    ends = [rows * k // pieces for k in range(pieces + 1)]
+    return [(low, high - low) for low, high in zip(ends[:-1], ends[1:])]
+
+
+LOW = 24
 HIGH = 16
 
 
 def block_kernel(
-    got_ref,
-    own_ref,
-    taps_ref,
-    low_gain_ref,
-    high_gain_ref,
+    got_hbm,
+    own_hbm,
+    taps_hbm,
+    low_gain_hbm,
+    high_gain_hbm,
     w_in_hbm,
     w_low_hbm,
     w_up_hbm,
     w_high_hbm,
     out_hbm,
+    got_ref,
+    near_ref,
+    own_ref,
+    taps_ref,
+    low_gain_ref,
+    high_gain_ref,
     w_in,
     w_low,
     w_up,
@@ -144,10 +155,12 @@
     a1_ref,
     a2_ref,
     low_ref,
+    lowf_ref,
     s1_ref,
     raw_ref,
     s2_ref,
     mix_ref,
+    done_ref,
     out_ref,
     in_sem,
     out_sem,
@@ -160,11 +173,30 @@
     copies.append(pltpu.make_async_copy(w_up_hbm, w_up, in_sem.at[5]))
     copies.append(pltpu.make_async_copy(w_high_hbm.at[0], w_high.at[0], in_sem.at[6]))
     copies.append(pltpu.make_async_copy(w_high_hbm.at[1], w_high.at[1], in_sem.at[7]))
+    small = [
+        pltpu.make_async_copy(source, target, in_sem.at[8 + n])
+        for n, (source, target) in enumerate(
+            (
+                (own_hbm, own_ref),
+                (taps_hbm, taps_ref),
+                (low_gain_hbm, low_gain_ref),
+                (high_gain_hbm, high_gain_ref),
+            )
+        )
+    ]
+    tokens = pltpu.make_async_copy(got_hbm.at[:, 0:8], got_ref, in_sem.at[12])
+    around = [(l, b) for b in (-1, 0, 1) for l in (-1, 0, 1) if l or b]
+    for n, (l, b) in enumerate(around):
+        source = lax.rem(lon + l + N_LON, N_LON) * N_BAND + lax.rem(band + b + N_BAND, N_BAND)
+        small.append(
+            pltpu.make_async_copy(got_hbm.at[source], near_ref.at[n], in_sem.at[13 + n])
+        )
+    for copy in [tokens] + small + copies:
+        copy.start()
     w_in[:, 48:128, :] = jnp.zeros((3, 80, CH), BF16)
-    for copy in copies:
-        copy.start()
-
-    tok_ref[...] = got_ref[:, 0:8, :].astype(F32).reshape(N_DEV * 8, 128)
+
+    tokens.wait()
+    tok_ref[...] = got_ref[...].astype(F32).reshape(N_DEV * 8, 128)
     x = jnp.concatenate([tok_ref[pl.ds(k, N_DEV, stride=8), :] for k in range(4)], axis=1)
     offset = lax.rem(LANES * lon + (128 - EDGE), 128)
     x = pltpu.roll(x, lax.rem(512 - offset, 512), axis=1)
@@ -179,9 +211,11 @@
     select = jnp.where(hit, 1.0, 0.0).T[:48].astype(BF16)
     latent = jnp.dot(select, x.astype(BF16), preferred_element_type=F32).astype(BF16)
 
+    for copy in small:
+        copy.wait()
+
     def chunk(d_lon, d_band):
-        source = lax.rem(lon + d_lon + N_LON, N_LON) * N_BAND + lax.rem(band + d_band + N_BAND, N_BAND)
-        return got_ref[source].astype(F32)[4:]
+        return near_ref[around.index((d_lon, d_band))].astype(F32)[4:]
 
     def side(d_lon):
         c = chunk(d_lon, 0)
@@ -214,38 +248,24 @@
     temporal = jnp.where(iota((48, 512), 1) < WINDOW, temporal, 0.0)
 
     wide = jnp.concatenate([temporal, jnp.zeros((48, 128), F32)], axis=1)
-    for j in range(24):
+    for j in range(LOW):
         piece = wide[:, 128 * (j // 8) : 128 * (j // 8) + 256]
         turn = LAT * (j % 8)
         if turn:
             piece = pltpu.roll(piece, 256 - turn, axis=1)
-        u_ref[j] = piece[:, :128]
-    lhs = jnp.concatenate(
-        [u_ref[:, p : p + 40, :].reshape(960, 128).astype(BF16) for p in range(3)], axis=1
-    )
-    for copy in copies[:3]:
-        copy.wait()
-    opening = jnp.dot(lhs, w_in[...].reshape(384, CH), preferred_element_type=F32)
-    opening = opening.astype(BF16).astype(F32)
-    for j in range(23):
-        for half in range(2):
-            open_ref[half, pl.ds(j, 40, stride=LOW), :] = opening[
-                40 * j : 40 * j + 40, 128 * half : 128 * half + 128
-            ]
-
-    def opened(rows):
-        return jnp.concatenate([open_ref[0, rows, :], open_ref[1, rows, :]], axis=1)
-
-    def zero_rows(ref, pitch, top, bottom):
-        total = ref.shape[0] // pitch
-
-        @pl.when(band == 0)
-        def _():
-            ref[0 : top * pitch, :] = jnp.zeros((top * pitch, ref.shape[1]), ref.dtype)
-
-        @pl.when(band == N_BAND - 1)
-        def _():
-            ref[(total - bottom) * pitch :, :] = jnp.zeros((bottom * pitch, ref.shape[1]), ref.dtype)
+        u_ref[pl.ds(j, 48, stride=LOW), :] = piece[:, :128]
+
+    def outside(value, pitch, row, top, bottom, rows):
+        count = value.shape[0] // pitch
+        above = min(max(top - row, 0), count)
+        below = min(max(row + count - (rows - bottom), 0), count)
+        parts = []
+        if above:
+            parts.append(jnp.where(band == 0, 0.0, value[: above * pitch]))
+        parts.append(value[above * pitch : (count - below) * pitch])
+        if below:
+            parts.append(jnp.where(band == N_BAND - 1, 0.0, value[(count - below) * pitch :]))
+        return parts[0] if len(parts) == 1 else jnp.concatenate(parts, axis=0)
 
     def conv(ref, pitch, row, count, lane, weight):
         total = None
@@ -258,111 +278,196 @@
             total = part if total is None else total + part
         return total
 
-    def spread(act, ref, at):
-        rows = slice(at, at + act.shape[0])
+    def spread(act, ref, row):
+        rows = slice(row * LOW, row * LOW + act.shape[0])
         ref[rows, 0:CH] = roll_rows(act, 1).astype(BF16)
         ref[rows, CH : 2 * CH] = act.astype(BF16)
         ref[rows, 2 * CH :] = roll_rows(act, -1).astype(BF16)
 
-    gain = low_gain_ref[0:1, :]
-    for r in range(0, 40, 10):
-        rows = slice(r * LOW, (r + 10) * LOW)
-        spread(activate(opened(rows), gain), a1_ref, r * LOW)
-    zero_rows(a1_ref, LOW, 4, 4)
-    copies[3].wait()
-    gain = low_gain_ref[1:2, :]
-    for r in range(0, 38, 19):
-        inner = conv(a1_ref, LOW, r, 19, 0, w_low.at[0])
-        spread(activate(inner, gain), a2_ref, r * LOW)
-    zero_rows(a2_ref, LOW, 3, 3)
-    copies[4].wait()
-    for r in range(0, 36, 18):
-        branch = conv(a2_ref, LOW, r, 18, 0, w_low.at[1])
-        low = opened(slice((r + 2) * LOW, (r + 20) * LOW)) + branch
-        for k in range(4):
-            part = roll_rows(low, -(2 + k)).reshape(18, LOW, CH)[:, :HIGH]
-            low_ref[r * HIGH : (r + 18) * HIGH, CH * k : CH * k + CH] = part.reshape(
-                18 * HIGH, CH
-            ).astype(BF16)
-    zero_rows(low_ref, HIGH, 2, 2)
-
-    copies[5].wait()
-    for a in range(2):
+    tasks = []
+
+    def task(product, finish, wait=None):
+        tasks.append((product, finish, wait))
+
+    for row, count in cuts(40, 4):
+
+        def product(row=row, count=count):
+            lhs = [u_ref[(row + p) * LOW : (row + p + count) * LOW, :] for p in range(3)]
+            lhs = jnp.concatenate(lhs, axis=1).astype(BF16)
+            return jnp.dot(lhs, w_in[...].reshape(384, CH), preferred_element_type=F32)
+
+        def finish(value, row=row, count=count):
+            value = value.astype(BF16).astype(F32)
+            open_ref[row * LOW : (row + count) * LOW, :] = value
+            act = activate(value, low_gain_ref[0:1, :])
+            spread(outside(act, LOW, row, 4, 4, 40), a1_ref, row)
+
+        task(product, finish, copies[:3] if row == 0 else None)
+
+    for row, count in cuts(38, 4):
+
+        def product(row=row, count=count):
+            return conv(a1_ref, LOW, row, count, 0, w_low.at[0])
+
+        def finish(value, row=row):
+            act = activate(value, low_gain_ref[1:2, :])
+            spread(outside(act, LOW, row, 3, 3, 38), a2_ref, row)
+
+        task(product, finish, copies[3:4] if row == 0 else None)
+
+    for row, count in cuts(36, 4):
+
+        def product(row=row, count=count):
+            return conv(a2_ref, LOW, row, count, 0, w_low.at[1])
+
+        def finish(value, row=row, count=count):
+            low = open_ref[(row + 2) * LOW : (row + 2 + count) * LOW, :] + value
+            low = outside(low.astype(BF16).astype(F32), LOW, row, 2, 2, 36)
+            for half in range(2):
+                lowf_ref[half, row * LOW : (row + count) * LOW, :] = low[
+                    :, 128 * half : 128 * half + 128
+                ]
+            for k in range(2):
+                part = roll_rows(low, -(3 + k)).reshape(count, LOW, CH)[:, :HIGH]
+                low_ref[row * HIGH : (row + count) * HIGH, CH * k : CH * k + CH] = part.reshape(
+                    count * HIGH, CH
+                ).astype(BF16)
+
+        task(product, finish, copies[4:5] if row == 0 else None)
+
+    def phase_weights(a, odd):
         for r in range(2):
             taps = ((0,), (1, 2)) if a == 0 else ((0, 1), (2,))
+            sides = ((0, 1), (2,)) if odd else ((0,), (1, 2))
+            for c in range(2):
+                total = None
+                for p in taps[r]:
+                    for q in sides[c]:
+                        one = w_up[3 * p + q].astype(F32)
+                        total = one if total is None else total + one
+                at = (2 * r + c) * CH
+                w_phase[a, odd, at : at + CH, :] = total.astype(BF16)
+
+    for n in (0, 17):
+        for a in range(2):
             for odd in range(2):
-                sides = ((0, 1), (2,)) if odd else ((0,), (1, 2))
-                for c in range(2):
-                    total = None
-                    for p in taps[r]:
-                        for q in sides[c]:
-                            one = w_up[3 * p + q].astype(F32)
-                            total = one if total is None else total + one
-                    w_phase[a, r, CH * c : CH * c + CH, (1 - odd) * CH : (2 - odd) * CH] = (
-                        total.astype(BF16)
-                    )
-    gain = high_gain_ref[0:1, :]
-    for a in range(2):
-        for n in range(0, 34, 17):
-
-            def phase(lane, out_lane, width):
-                total = None
-                for r in range(2):
-                    at = (n + a + r) * HIGH
-                    part = jnp.dot(
-                        low_ref[at : at + 17 * HIGH, lane : lane + 2 * CH],
-                        w_phase[a, r, :, out_lane : out_lane + width],
+
+                def product(n=n, a=a, odd=odd):
+                    parts = []
+                    for r in range(2):
+                        at = n + a + r
+                        col = 19 if odd else 2
+                        pair = [
+                            lowf_ref[half, pl.ds(at * LOW + col + c, 24, stride=LOW), :]
+                            for c in range(2)
+                            for half in range(2)
+                        ]
+                        pair = jnp.concatenate(pair, axis=1).astype(BF16)
+                        main = low_ref[at * HIGH : (at + 17) * HIGH, :]
+                        pad = jnp.zeros((8, 2 * CH), BF16)
+                        parts.append(jnp.concatenate([main, pair, pad], axis=0))
+                    return jnp.dot(
+                        jnp.concatenate(parts, axis=1),
+                        w_phase[a, odd],
                         preferred_element_type=F32,
                     )
-                    total = part if total is None else total + part
-                return total.astype(BF16).astype(F32)
-
-            def put(value, slot, raw_slot):
-                act = activate(value, gain).astype(BF16)
-                raw = value.astype(BF16)
-                for i in range(17):
-                    at = (2 * (n + i) + a) * HIGH
-                    rows = slice(i * HIGH, (i + 1) * HIGH)
-                    s1_ref[at : at + HIGH, CH * slot : CH * slot + CH] = act[rows]
-                    if raw_slot is not None:
-                        raw_ref[at : at + HIGH, CH * raw_slot : CH * raw_slot + CH] = raw[rows]
-
-            both = phase(CH, 0, 2 * CH)
-            put(both[:, :CH], 1, None)
-            put(both[:, CH:], 2, 0)
-            put(phase(2 * CH, 0, CH), 3, 1)
-            put(phase(0, CH, CH), 0, None)
-    zero_rows(s1_ref, HIGH, 2, 2)
-
-    copies[6].wait()
-    gain = high_gain_ref[1:2, :]
-    for r in range(0, 66, 22):
-        rows = slice(r * HIGH, (r + 22) * HIGH)
-        odd = activate(conv(s1_ref, HIGH, r, 22, 0, w_high.at[0]), gain)
-        s2_ref[rows, 0:CH] = odd.astype(BF16)
-        s2_ref[rows, 2 * CH : 3 * CH] = roll_rows(odd, -1).astype(BF16)
-        even = activate(conv(s1_ref, HIGH, r, 22, CH, w_high.at[0]), gain)
-        s2_ref[rows, CH : 2 * CH] = even.astype(BF16)
-        s2_ref[rows, 3 * CH :] = roll_rows(even, -1).astype(BF16)
-    zero_rows(s2_ref, HIGH, 1, 1)
-    copies[7].wait()
+
+                def finish(value, n=n, a=a, odd=odd):
+                    value = value[: 17 * HIGH + 24].astype(BF16)
+                    act = activate(value.astype(F32), high_gain_ref[0:1, :])
+                    border = act[17 * HIGH :]
+                    act = act[: 17 * HIGH]
+                    turned = roll_rows(act, -1 if odd else 1)
+                    for half in range(2):
+                        lanes = slice(128 * half, 128 * half + 128)
+                        mix_ref[odd, half, 0 : 17 * HIGH, :] = turned[:, lanes]
+                        mix_ref[odd, half, pl.ds(15 if odd else 0, 24, stride=HIGH), :] = border[
+                            :, lanes
+                        ]
+                    turned = jnp.concatenate(
+                        [mix_ref[odd, half, 0 : 17 * HIGH, :] for half in range(2)], axis=1
+                    )
+                    act = outside(act, HIGH, n, 1, 1, 34).astype(BF16)
+                    turned = outside(turned, HIGH, n, 1, 1, 34).astype(BF16)
+                    slot, beside = (1, 3) if odd else (2, 0)
+                    for i in range(17):
+                        rows = slice(i * HIGH, (i + 1) * HIGH)
+                        at = (2 * (n + i) + a) * HIGH
+                        s1_ref[at : at + HIGH, CH * slot : CH * slot + CH] = act[rows]
+                        s1_ref[at : at + HIGH, CH * beside : CH * beside + CH] = turned[rows]
+                        raw_ref[at : at + HIGH, CH * odd : CH * odd + CH] = value[rows]
+
+                task(product, finish)
+
+    for row, count in cuts(66, 6):
+        for odd in range(2):
+
+            def product(row=row, count=count, odd=odd):
+                return conv(s1_ref, HIGH, row, count, 0 if odd else CH, w_high.at[0])
+
+            def finish(value, row=row, count=count, odd=odd):
+                act = activate(value, high_gain_ref[1:2, :])
+                act = outside(act, HIGH, row, 1, 1, 66)
+                slot, beside = (1, 3) if odd else (2, 0)
+                rows = slice(row * HIGH, (row + count) * HIGH)
+                s2_ref[rows, CH * slot : CH * slot + CH] = act.astype(BF16)
+                s2_ref[rows, CH * beside : CH * beside + CH] = roll_rows(
+                    act, -1 if odd else 1
+                ).astype(BF16)
+
+            task(product, finish, copies[6:7] if row == 0 and odd == 0 else None)
+
+    turn = iota((256, 256), 0)
+    turn = jnp.where(
+        iota((256, 256), 1) == (turn % 16) * HIGH + turn // 16, 1.0, 0.0
+    ).astype(BF16)
     outs = []
-    for n, r in enumerate(range(0, 64, 16)):
-        rows = slice((r + 2) * HIGH, (r + 18) * HIGH)
-        even = conv(s2_ref, HIGH, r, 16, 0, w_high.at[1]) + raw_ref[rows, :CH].astype(F32)
-        odd = conv(s2_ref, HIGH, r, 16, CH, w_high.at[1]) + raw_ref[rows, CH:].astype(F32)
-        for half in range(2):
-            lanes = slice(128 * half, 128 * half + 128)
-            mix_ref[n % 2, half, pl.ds(0, 16 * HIGH, stride=2), :] = even[:, lanes]
-            mix_ref[n % 2, half, pl.ds(1, 16 * HIGH, stride=2), :] = odd[:, lanes]
-            out_ref[r : r + 16, :, lanes] = (
-                mix_ref[n % 2, half].astype(BF16).reshape(16, 32, 128)[:, :30]
-            )
-        copy = pltpu.make_async_copy(
-            out_ref.at[r : r + 16], out_hbm.at[r : r + 16], out_sem.at[n]
-        )
-        copy.start()
-        outs.append(copy)
+    late = []
+    for n, row in enumerate(range(0, 64, 16)):
+        for odd in range(2):
+
+            def product(row=row, odd=odd):
+                return conv(s2_ref, HIGH, row, 16, 0 if odd else CH, w_high.at[1])
+
+            def finish(value, row=row, odd=odd):
+                rows = slice((row + 2) * HIGH, (row + 18) * HIGH)
+                value = value + raw_ref[rows, odd * CH : odd * CH + CH].astype(F32)
+                done_ref[odd] = value.astype(BF16)
+
+            def turned(odd=odd):
+                return jnp.dot(turn, done_ref[odd], preferred_element_type=F32)
+
+            def put(value, n=n, row=row, odd=odd):
+                value = value.astype(BF16)
+                for j in range(COLS):
+                    at = (j + odd) * 16
+                    out_ref[2 * j + odd, row : row + 16, :] = value[at : at + 16]
+                if odd:
+                    copy = pltpu.make_async_copy(
+                        out_ref.at[:, row : row + 16], out_hbm.at[:, row : row + 16], out_sem.at[n]
+                    )
+                    copy.start()
+                    outs.append(copy)
+
+            task(product, finish, copies[7:8] if row == 0 and odd == 0 else None)
+            late.append((turned, put))
+            if len(late) > 1:
+                task(*late.pop(0))
+    task(*late.pop(0))
+
+    before = None
+    for number, (product, finish, wait) in enumerate(tasks):
+        for copy in wait or ():
+            copy.wait()
+        value = product()
+        if before is not None:
+            before[0](before[1])
+        before = (finish, value)
+        if number == 5:
+            copies[5].wait()
+        if 5 <= number <= 8:
+            phase_weights((number - 5) // 2, (number - 5) % 2)
+    before[0](before[1])
     for copy in outs:
         copy.wait()
 
@@ -383,7 +488,7 @@
     struct = jax.ShapeDtypeStruct
     vmem = pl.BlockSpec(memory_space=pltpu.VMEM)
     smem = pl.BlockSpec(memory_space=pltpu.SMEM)
-    anywhere = pl.BlockSpec(memory_space=pl.ANY)
+    hbm = pl.BlockSpec(memory_space=pltpu.HBM)
     payload, own = pl.pallas_call(
         pack_kernel,
         in_specs=[smem, smem, vmem, vmem, vmem],
@@ -399,32 +504,40 @@
         temporal_taps_weight,
     )
     arrived = lax.all_to_all(payload, ("lon", "band"), 0, 0, tiled=True)
-    return pl.pallas_call(
+    decoded = pl.pallas_call(
         block_kernel,
-        in_specs=[vmem] * 5 + [anywhere] * 4,
-        out_specs=anywhere,
-        out_shape=struct((2 * ROWS, 2 * COLS, CH), BF16),
+        in_specs=[hbm] * 9,
+        out_specs=hbm,
+        out_shape=struct((2 * COLS, 2 * ROWS, CH), BF16),
         scratch_shapes=[
+            pltpu.VMEM((N_DEV, 8, 128), BF16),
+            pltpu.VMEM((8, CHUNK, 128), BF16),
+            pltpu.VMEM((ROWS, 256), F32),
+            pltpu.VMEM((3, LAT, LAT), BF16),
+            pltpu.VMEM((2, CH), F32),
+            pltpu.VMEM((2, CH), F32),
             pltpu.VMEM((3, 128, CH), BF16),
             pltpu.VMEM((2, 3, 3 * CH, CH), BF16),
             pltpu.VMEM((9, CH, CH), BF16),
             pltpu.VMEM((2, 3, 3 * CH, CH), BF16),
-            pltpu.VMEM((2, 2, 2 * CH, 2 * CH), BF16),
+            pltpu.VMEM((2, 2, 4 * CH, CH), BF16),
             pltpu.VMEM((N_DEV * 8, 128), F32),
-            pltpu.VMEM((24, 48, 128), F32),
-            pltpu.VMEM((2, 40 * LOW, 128), F32),
+            pltpu.VMEM((48 * LOW, 128), F32),
+            pltpu.VMEM((40 * LOW, CH), F32),
             pltpu.VMEM((40 * LOW, 3 * CH), BF16),
             pltpu.VMEM((38 * LOW, 3 * CH), BF16),
-            pltpu.VMEM((36 * HIGH, 4 * CH), BF16),
+            pltpu.VMEM((36 * HIGH, 2 * CH), BF16),
+            pltpu.VMEM((2, 44 * LOW, 128), F32),
             pltpu.VMEM((68 * HIGH, 4 * CH), BF16),
             pltpu.VMEM((68 * HIGH, 2 * CH), BF16),
             pltpu.VMEM((66 * HIGH, 4 * CH), BF16),
-            pltpu.VMEM((2, 2, 2 * 16 * HIGH, 128), F32),
-            pltpu.VMEM((2 * ROWS, 2 * COLS, CH), BF16),
-            pltpu.SemaphoreType.DMA((8,)),
+            pltpu.VMEM((2, 2, 24 * HIGH, 128), F32),
+            pltpu.VMEM((2, 256, CH), BF16),
+            pltpu.VMEM((2 * COLS, 2 * ROWS, CH), BF16),
+            pltpu.SemaphoreType.DMA((21,)),
             pltpu.SemaphoreType.DMA((4,)),
         ],
-        compiler_params=pltpu.CompilerParams(vmem_limit_bytes=50 * 1024 * 1024),
+        compiler_params=pltpu.CompilerParams(vmem_limit_bytes=56 * 1024 * 1024),
         name="block",
     )(
         arrived,
@@ -437,6 +550,7 @@
         upsampled_weight,
         upper_conv_weights.reshape(2, 3, 3 * CH, CH),
     )
+    return decoded.transpose(1, 0, 2)
 
 
 def solution(mesh):

time: 53.2 us -> 45.8 us (0.86)
  local copies, waits for them, and re-layouts: 5.21 us -> 0 us
  Pallas kernels: 19.5 us -> 17.3 us
    unnamed x12 -> x0, local copies, waits for them, and re-layouts: 3.71 us -> none
    pallas_call x1, Pallas kernels: 17.1 us -> 15.1 us  [shards(): pl.pallas_call(block_kernel, in_specs=[hbm] * 9, out_specs=hbm, out_shape...]
    pallas_call x1 -> x0, local copies, waits for them, and re-layouts: 1.49 us -> none  [shards(): pl.pallas_call(block_kernel, in_specs=[vmem] * 5 + [anywhere] * 4, out_sp...]
where the time goes in v1:
time: 45.8 us; the launch traced here: 45.6 us
  blocking collectives  28.2 us (62%)
  Pallas kernels  17.3 us (38%)
    all_to_all x1, blocking collectives, shards(): arrived = lax.all_to_all(payload, ('lon', 'band'), 0, 0, tiled=True)  28.2 us
    pallas_call x1, Pallas kernels, shards(): pl.pallas_call(block_kernel, in_specs=[hbm] * 9, out_specs=hbm, out_shape...  15.1 us
    pallas_call x1, Pallas kernels, shards(): pl.pallas_call(pack_kernel, in_specs=[smem, smem, vmem, vmem, vmem], out_...  2.24 us

profile of v1, /device:TPU:1, one launch (start us, length us, event | category | flops | bytes accessed | tf_op | source)
XLA Modules:
  0.0 45.6 jit_solution(173560794223946334)
XLA Ops:
  0.0 2.2 %pack.1 = (bf16[128,24,128]{2,1,0:T(8,128)(2,1)}, f32[32,256]{1,0:T(8,128)}) custom-call(s32[1,32]{1,0:T(1,128)} %index_ref.1, s32[4]{0:T(128)} %slot_ref.1, bf16[1,1,7680]{2,1,0:T(2,128)(2,1)} %token_ref.1, bf16[4,32,240]{2,1,0:T(8,128)(2,1)} %cache_ref.1, bf16[3,16,16]{2,1,0:T(8,128)(2,1)} %taps_hbm.1), custom_call_target="tpu_custom_call" | custom-call | tf_op jit(solution)/shard_map/pack/pallas_call | solution.py:492
  2.2 28.2 %all_to_all.5.got_hbm = bf16[128,24,128]{2,1,0:T(8,128)(2,1)} all-to-all(bf16[128,24,128]{2,1,0:T(8,128)(2,1)} %get-tuple-element.7), channel_id=1, replica_groups=mesh['lon'=32,'band'=4] {'lon','band'}, dimensions={0} | all-to-all | bytes 1572864 | tf_op jit(solution)/shard_map/all_to_all | solution.py:506
  30.5 15.1 %block.1 = bf16[30,64,256]{2,1,0:T(8,128)(2,1)} custom-call(bf16[128,24,128]{2,1,0:T(8,128)(2,1)} %all_to_all.5.got_hbm, f32[32,256]{1,0:T(8,128)} %get-tuple-element.8.own_hbm, bf16[3,16,16]{2,1,0:T(8,128)(2,1)} %taps_hbm.1, f32[2,256]{1,0:T(2,128)} %low_gain_hbm.1, f32[2,256]{1,0:T(2,128)} %high_gain_hbm.1, bf16[3,48,256]{2,1,0:T(8,128)(2,1)} %bitcast.6, ...), custom_call_target="tpu_custom_call" | custom-call | tf_op jit(solution)/shard_map/block/pallas_call | solution.py:507

commit v2 on v1

--- a/solution.py
+++ b/solution.py
@@ -12,7 +12,6 @@
 
 N_LON = 32
 N_BAND = 4
-N_DEV = N_LON * N_BAND
 ROWS = 32
 COLS = 15
 LAT = 16
@@ -48,7 +47,6 @@
 
 def pack_kernel(index_ref, slot_ref, token_ref, cache_ref, taps_ref, send_ref, own_ref, x_ref):
     lon = lax.axis_index("lon")
-    band = lax.axis_index("band")
     row = jnp.int32(0)
     for r in range(ROWS):
         row = jnp.where(index_ref[0, r] == lon, r, row)
@@ -63,9 +61,7 @@
         start = window_start(target) % 60
         spot = (window_offset(target) + WINDOW) % 512
         tile = x_ref[start : start + 8, :]
-        tile = jnp.where(place == spot, tag, tile).astype(BF16)
-        for b in range(N_BAND):
-            send_ref[target * N_BAND + b, 0:8, :] = tile
+        send_ref[target, 0:8, :] = jnp.where(place == spot, tag, tile).astype(BF16)
 
     diagonals = [block_diagonal(taps_ref[t]) for t in (1, 2)]
     mixed = jnp.zeros((2 * ROWS, 128), F32)
@@ -77,35 +73,72 @@
     own = jnp.concatenate([mixed[:ROWS], mixed[ROWS:]], axis=1)
     own_ref[...] = own
 
-    def send(d_lon, d_band, part):
-        rest = CHUNK - 4 - part.shape[0]
-        full = [jnp.zeros((4, 128), F32), part]
-        if rest:
-            full.append(jnp.zeros((rest, 128), F32))
-        full = jnp.concatenate(full, axis=0)
-        to = lax.rem(lon + d_lon + N_LON, N_LON) * N_BAND + lax.rem(band + d_band + N_BAND, N_BAND)
+    for d_lon, v in ((-1, own[:, :EDGE]), (1, own[:, LANES - EDGE : LANES])):
+        top = jnp.concatenate([v[:16, :], v[16:, : 128 - EDGE]], axis=1)
+        low = jnp.concatenate(
+            [v[16 + 4 * m : 20 + 4 * m, 128 - EDGE : EDGE] for m in range(4)], axis=1
+        )
+        full = jnp.concatenate([jnp.zeros((4, 128), F32), top, low], axis=0)
+        to = lax.rem(lon + d_lon + N_LON, N_LON)
         first = send_ref[to, 0:8, :].astype(F32)
         send_ref[to, 0:8, :] = jnp.where(iota((8, 128), 0) < 4, first, full[:8]).astype(BF16)
         send_ref[to, 8:CHUNK, :] = full[8:].astype(BF16)
 
-    def tall(v):
-        top = jnp.concatenate([v[:16, :EDGE], v[16:, : 128 - EDGE]], axis=1)
-        low = jnp.concatenate(
-            [v[16 + 4 * m : 20 + 4 * m, 128 - EDGE : EDGE] for m in range(4)], axis=1
-        )
-        return jnp.concatenate([top, low], axis=0)
-
-    def corner(v):
-        return jnp.concatenate([v, jnp.zeros((HALO, 128 - EDGE), F32)], axis=1)
-
-    left, right = own[:, :EDGE], own[:, LANES - EDGE : LANES]
-    send(-1, 0, tall(left))
-    send(1, 0, tall(right))
-    for d_band, rows in ((-1, slice(0, HALO)), (1, slice(ROWS - HALO, ROWS))):
-        wide = own[rows]
-        send(0, d_band, jnp.concatenate([wide[:, :128], wide[:, 128:]], axis=0))
-        send(-1, d_band, corner(left[rows]))
-        send(1, d_band, corner(right[rows]))
+
+def mix_kernel(
+    got_hbm,
+    own_hbm,
+    taps_hbm,
+    out_ref,
+    first_ref,
+    last_ref,
+    got_ref,
+    near_ref,
+    own_ref,
+    taps_ref,
+    tok_ref,
+    sem,
+):
+    lon = lax.axis_index("lon")
+    copies = [
+        pltpu.make_async_copy(got_hbm.at[:, 0:8], got_ref, sem.at[0]),
+        pltpu.make_async_copy(taps_hbm, taps_ref, sem.at[1]),
+        pltpu.make_async_copy(own_hbm, own_ref, sem.at[2]),
+    ]
+    for n in range(2):
+        source = lax.rem(lon + 2 * n - 1 + N_LON, N_LON)
+        copies.append(pltpu.make_async_copy(got_hbm.at[source], near_ref.at[n], sem.at[3 + n]))
+    for copy in copies:
+        copy.start()
+    for copy in copies:
+        copy.wait()
+
+    tok_ref[...] = got_ref[...].astype(F32).reshape(N_LON * 8, 128)
+    x = jnp.concatenate([tok_ref[pl.ds(k, N_LON, stride=8), :] for k in range(4)], axis=1)
+    offset = lax.rem(LANES * lon + (128 - EDGE), 128)
+    x = pltpu.roll(x, lax.rem(512 - offset, 512), axis=1)
+    tag = x[:, WINDOW : WINDOW + 1].astype(jnp.int32)
+    select = jnp.where(tag == iota((N_LON, 128), 1), 1.0, 0.0)
+    select = jnp.concatenate([select, jnp.zeros((128 - N_LON, 128), F32)], axis=0)
+    select = select.T[:ROWS, :N_LON].astype(BF16)
+    latent = jnp.dot(select, x.astype(BF16), preferred_element_type=F32).astype(BF16)
+
+    def side(n):
+        c = near_ref[n].astype(F32)[4:]
+        low = jnp.concatenate([c[16:20, 32 * k : 32 * k + 32] for k in range(4)], axis=0)
+        low = jnp.concatenate([c[:16, EDGE:], low], axis=1)
+        return jnp.concatenate([c[:16, :EDGE], low], axis=0)
+
+    cached = jnp.concatenate(
+        [side(0), own_ref[:, :LANES], side(1), jnp.zeros((ROWS, 512 - WINDOW), F32)], axis=1
+    )
+    stacked = jnp.concatenate([latent[:, 128 * k : 128 * k + 128] for k in range(4)], axis=0)
+    fresh = jnp.dot(stacked, block_diagonal(taps_ref[0]), preferred_element_type=F32)
+    fresh = jnp.concatenate([fresh[ROWS * k : ROWS * k + ROWS] for k in range(4)], axis=1)
+    temporal = jnp.where(iota((ROWS, 512), 1) < WINDOW, fresh + cached, 0.0)
+    out_ref[...] = temporal.astype(BF16)
+    first_ref[...] = temporal[:8].astype(BF16)
+    last_ref[...] = temporal[ROWS - 8 :].astype(BF16)
 
 
 def activate(values, gain):
@@ -128,9 +161,9 @@
 
 
 def block_kernel(
-    got_hbm,
-    own_hbm,
-    taps_hbm,
+    temporal_hbm,
+    above_hbm,
+    below_hbm,
     low_gain_hbm,
     high_gain_hbm,
     w_in_hbm,
@@ -138,10 +171,8 @@
     w_up_hbm,
     w_high_hbm,
     out_hbm,
-    got_ref,
-    near_ref,
-    own_ref,
-    taps_ref,
+    temporal_ref,
+    rim_ref,
     low_gain_ref,
     high_gain_ref,
     w_in,
@@ -149,7 +180,6 @@
     w_up,
     w_high,
     w_phase,
-    tok_ref,
     u_ref,
     open_ref,
     a1_ref,
@@ -160,12 +190,10 @@
     raw_ref,
     s2_ref,
     mix_ref,
-    done_ref,
     out_ref,
     in_sem,
     out_sem,
 ):
-    lon = lax.axis_index("lon")
     band = lax.axis_index("band")
     copies = [pltpu.make_async_copy(w_in_hbm.at[p], w_in.at[p, 0:48], in_sem.at[p]) for p in range(3)]
     copies.append(pltpu.make_async_copy(w_low_hbm.at[0], w_low.at[0], in_sem.at[3]))
@@ -177,75 +205,31 @@
         pltpu.make_async_copy(source, target, in_sem.at[8 + n])
         for n, (source, target) in enumerate(
             (
-                (own_hbm, own_ref),
-                (taps_hbm, taps_ref),
+                (temporal_hbm, temporal_ref),
+                (above_hbm, rim_ref.at[0]),
+                (below_hbm, rim_ref.at[1]),
                 (low_gain_hbm, low_gain_ref),
                 (high_gain_hbm, high_gain_ref),
             )
         )
     ]
-    tokens = pltpu.make_async_copy(got_hbm.at[:, 0:8], got_ref, in_sem.at[12])
-    around = [(l, b) for b in (-1, 0, 1) for l in (-1, 0, 1) if l or b]
-    for n, (l, b) in enumerate(around):
-        source = lax.rem(lon + l + N_LON, N_LON) * N_BAND + lax.rem(band + b + N_BAND, N_BAND)
-        small.append(
-            pltpu.make_async_copy(got_hbm.at[source], near_ref.at[n], in_sem.at[13 + n])
-        )
-    for copy in [tokens] + small + copies:
+    for copy in small + copies:
         copy.start()
     w_in[:, 48:128, :] = jnp.zeros((3, 80, CH), BF16)
 
-    tokens.wait()
-    tok_ref[...] = got_ref[...].astype(F32).reshape(N_DEV * 8, 128)
-    x = jnp.concatenate([tok_ref[pl.ds(k, N_DEV, stride=8), :] for k in range(4)], axis=1)
-    offset = lax.rem(LANES * lon + (128 - EDGE), 128)
-    x = pltpu.roll(x, lax.rem(512 - offset, 512), axis=1)
-    tag = x[:, WINDOW : WINDOW + 1].astype(jnp.int32)
-    m = iota((N_DEV, 128), 1)
-    want_band = jnp.where(m < HALO, band - 1, jnp.where(m < HALO + ROWS, band, band + 1))
-    want_row = jnp.where(
-        m < HALO, m + ROWS - HALO, jnp.where(m < HALO + ROWS, m - HALO, m - HALO - ROWS)
-    )
-    want_row = jnp.where(m < 2 * HALO + ROWS, want_row, -1)
-    hit = (tag == want_row) & (iota((N_DEV, 128), 0) % N_BAND == want_band)
-    select = jnp.where(hit, 1.0, 0.0).T[:48].astype(BF16)
-    latent = jnp.dot(select, x.astype(BF16), preferred_element_type=F32).astype(BF16)
-
     for copy in small:
         copy.wait()
-
-    def chunk(d_lon, d_band):
-        return near_ref[around.index((d_lon, d_band))].astype(F32)[4:]
-
-    def side(d_lon):
-        c = chunk(d_lon, 0)
-        low = jnp.concatenate([c[16:20, 32 * k : 32 * k + 32] for k in range(4)], axis=0)
-        low = jnp.concatenate([c[:16, EDGE:], low], axis=1)
-        return jnp.concatenate([c[:16, :EDGE], low], axis=0)
-
-    def rim(d_band):
-        c = chunk(0, d_band)
-        parts = [
-            chunk(-1, d_band)[:HALO, :EDGE],
-            c[:HALO],
-            c[HALO : 2 * HALO, : LANES - 128],
-            chunk(1, d_band)[:HALO, :EDGE],
-            jnp.zeros((HALO, 512 - WINDOW), F32),
-        ]
-        whole = jnp.concatenate(parts, axis=1)
-        inside = (band + d_band >= 0) & (band + d_band < N_BAND)
-        return jnp.where(inside, whole, 0.0)
-
-    middle = jnp.concatenate(
-        [side(-1), own_ref[:, :LANES], side(1), jnp.zeros((ROWS, 512 - WINDOW), F32)], axis=1
+    above = jnp.where(band > 0, rim_ref[0].astype(F32), 0.0)
+    below = jnp.where(band < N_BAND - 1, rim_ref[1].astype(F32), 0.0)
+    temporal = jnp.concatenate(
+        [
+            above[8 - HALO :],
+            temporal_ref[...].astype(F32),
+            below[:HALO],
+            jnp.zeros((6, 512), F32),
+        ],
+        axis=0,
     )
-    cached = jnp.concatenate([rim(-1), middle, rim(1), jnp.zeros((6, 512), F32)], axis=0)
-    diagonal = block_diagonal(taps_ref[0])
-    stacked = jnp.concatenate([latent[:, 128 * k : 128 * k + 128] for k in range(4)], axis=0)
-    fresh = jnp.dot(stacked, diagonal, preferred_element_type=F32)
-    fresh = jnp.concatenate([fresh[48 * k : 48 * k + 48] for k in range(4)], axis=1)
-    temporal = (fresh + cached).astype(BF16).astype(F32)
-    temporal = jnp.where(iota((48, 512), 1) < WINDOW, temporal, 0.0)
 
     wide = jnp.concatenate([temporal, jnp.zeros((48, 128), F32)], axis=1)
     for j in range(LOW):
@@ -289,7 +273,7 @@
     def task(product, finish, wait=None):
         tasks.append((product, finish, wait))
 
-    for row, count in cuts(40, 4):
+    for row, count in cuts(40, 3):
 
         def product(row=row, count=count):
             lhs = [u_ref[(row + p) * LOW : (row + p + count) * LOW, :] for p in range(3)]
@@ -304,7 +288,7 @@
 
         task(product, finish, copies[:3] if row == 0 else None)
 
-    for row, count in cuts(38, 4):
+    for row, count in cuts(38, 3):
 
         def product(row=row, count=count):
             return conv(a1_ref, LOW, row, count, 0, w_low.at[0])
@@ -315,7 +299,7 @@
 
         task(product, finish, copies[3:4] if row == 0 else None)
 
-    for row, count in cuts(36, 4):
+    for row, count in cuts(36, 3):
 
         def product(row=row, count=count):
             return conv(a2_ref, LOW, row, count, 0, w_low.at[1])
@@ -417,31 +401,19 @@
 
             task(product, finish, copies[6:7] if row == 0 and odd == 0 else None)
 
-    turn = iota((256, 256), 0)
-    turn = jnp.where(
-        iota((256, 256), 1) == (turn % 16) * HIGH + turn // 16, 1.0, 0.0
-    ).astype(BF16)
     outs = []
-    late = []
     for n, row in enumerate(range(0, 64, 16)):
         for odd in range(2):
 
             def product(row=row, odd=odd):
                 return conv(s2_ref, HIGH, row, 16, 0 if odd else CH, w_high.at[1])
 
-            def finish(value, row=row, odd=odd):
+            def finish(value, n=n, row=row, odd=odd):
                 rows = slice((row + 2) * HIGH, (row + 18) * HIGH)
                 value = value + raw_ref[rows, odd * CH : odd * CH + CH].astype(F32)
-                done_ref[odd] = value.astype(BF16)
-
-            def turned(odd=odd):
-                return jnp.dot(turn, done_ref[odd], preferred_element_type=F32)
-
-            def put(value, n=n, row=row, odd=odd):
-                value = value.astype(BF16)
+                value = jnp.swapaxes(value.reshape(16, HIGH, CH), 0, 1).astype(BF16)
                 for j in range(COLS):
-                    at = (j + odd) * 16
-                    out_ref[2 * j + odd, row : row + 16, :] = value[at : at + 16]
+                    out_ref[2 * j + odd, row : row + 16, :] = value[j + odd]
                 if odd:
                     copy = pltpu.make_async_copy(
                         out_ref.at[:, row : row + 16], out_hbm.at[:, row : row + 16], out_sem.at[n]
@@ -450,10 +422,6 @@
                     outs.append(copy)
 
             task(product, finish, copies[7:8] if row == 0 and odd == 0 else None)
-            late.append((turned, put))
-            if len(late) > 1:
-                task(*late.pop(0))
-    task(*late.pop(0))
 
     before = None
     for number, (product, finish, wait) in enumerate(tasks):
@@ -463,10 +431,10 @@
         if before is not None:
             before[0](before[1])
         before = (finish, value)
-        if number == 5:
+        if number == 4:
             copies[5].wait()
-        if 5 <= number <= 8:
-            phase_weights((number - 5) // 2, (number - 5) % 2)
+        if 4 <= number <= 7:
+            phase_weights((number - 4) // 2, (number - 4) % 2)
     before[0](before[1])
     for copy in outs:
         copy.wait()
@@ -489,11 +457,12 @@
     vmem = pl.BlockSpec(memory_space=pltpu.VMEM)
     smem = pl.BlockSpec(memory_space=pltpu.SMEM)
     hbm = pl.BlockSpec(memory_space=pltpu.HBM)
+    anywhere = pl.BlockSpec(memory_space=pl.ANY)
     payload, own = pl.pallas_call(
         pack_kernel,
         in_specs=[smem, smem, vmem, vmem, vmem],
         out_specs=[vmem, vmem],
-        out_shape=[struct((N_DEV, CHUNK, 128), BF16), struct((ROWS, 256), F32)],
+        out_shape=[struct((N_LON, CHUNK, 128), BF16), struct((ROWS, 256), F32)],
         scratch_shapes=[pltpu.VMEM((72, 128), F32)],
         name="pack",
     )(
@@ -503,17 +472,34 @@
         latent_frame_cache,
         temporal_taps_weight,
     )
-    arrived = lax.all_to_all(payload, ("lon", "band"), 0, 0, tiled=True)
+    arrived = lax.all_to_all(payload, "lon", 0, 0, tiled=True)
+    temporal, first, last = pl.pallas_call(
+        mix_kernel,
+        in_specs=[hbm] * 3,
+        out_specs=[vmem] * 3,
+        out_shape=[struct((ROWS, 512), BF16), struct((8, 512), BF16), struct((8, 512), BF16)],
+        scratch_shapes=[
+            pltpu.VMEM((N_LON, 8, 128), BF16),
+            pltpu.VMEM((2, CHUNK, 128), BF16),
+            pltpu.VMEM((ROWS, 256), F32),
+            pltpu.VMEM((3, LAT, LAT), BF16),
+            pltpu.VMEM((N_LON * 8, 128), F32),
+            pltpu.SemaphoreType.DMA((5,)),
+        ],
+        compiler_params=pltpu.CompilerParams(vmem_limit_bytes=56 * 1024 * 1024),
+        name="mix",
+    )(arrived, own, temporal_taps_weight)
+    ring = [(b, (b + 1) % N_BAND) for b in range(N_BAND)]
+    above = lax.ppermute(last, "band", ring)
+    below = lax.ppermute(first, "band", [(b, a) for a, b in ring])
     decoded = pl.pallas_call(
         block_kernel,
-        in_specs=[hbm] * 9,
+        in_specs=[anywhere] * 3 + [hbm] * 6,
         out_specs=hbm,
         out_shape=struct((2 * COLS, 2 * ROWS, CH), BF16),
         scratch_shapes=[
-            pltpu.VMEM((N_DEV, 8, 128), BF16),
-            pltpu.VMEM((8, CHUNK, 128), BF16),
-            pltpu.VMEM((ROWS, 256), F32),
-            pltpu.VMEM((3, LAT, LAT), BF16),
+            pltpu.VMEM((ROWS, 512), BF16),
+            pltpu.VMEM((2, 8, 512), BF16),
             pltpu.VMEM((2, CH), F32),
             pltpu.VMEM((2, CH), F32),
             pltpu.VMEM((3, 128, CH), BF16),
@@ -521,7 +507,6 @@
             pltpu.VMEM((9, CH, CH), BF16),
             pltpu.VMEM((2, 3, 3 * CH, CH), BF16),
             pltpu.VMEM((2, 2, 4 * CH, CH), BF16),
-            pltpu.VMEM((N_DEV * 8, 128), F32),
             pltpu.VMEM((48 * LOW, 128), F32),
             pltpu.VMEM((40 * LOW, CH), F32),
             pltpu.VMEM((40 * LOW, 3 * CH), BF16),
@@ -532,17 +517,16 @@
             pltpu.VMEM((68 * HIGH, 2 * CH), BF16),
             pltpu.VMEM((66 * HIGH, 4 * CH), BF16),
             pltpu.VMEM((2, 2, 24 * HIGH, 128), F32),
-            pltpu.VMEM((2, 256, CH), BF16),
             pltpu.VMEM((2 * COLS, 2 * ROWS, CH), BF16),
-            pltpu.SemaphoreType.DMA((21,)),
+            pltpu.SemaphoreType.DMA((13,)),
             pltpu.SemaphoreType.DMA((4,)),
         ],
         compiler_params=pltpu.CompilerParams(vmem_limit_bytes=56 * 1024 * 1024),
         name="block",
     )(
-        arrived,
-        own,
-        temporal_taps_weight,
+        temporal,
+        above,
+        below,
         latent_norm_gains,
         upper_norm_gains,
         input_weight.reshape(3, 48, CH),

time: 45.8 us -> 44.6 us (0.974)
  blocking collectives: 28.2 us -> 20.8 us
  waiting for transfers between devices: 0 us -> 3.28 us
  starting transfers between devices: 0 us -> 2.33 us
  local copies, waits for them, and re-layouts: 0 us -> 0.6 us
    all_to_all x1, blocking collectives: 28.2 us -> 20.8 us  [shards(): arrived = lax.all_to_all(payload, 'lon', 0, 0, tiled=True)]
    ppermute x0 -> x2, waiting for transfers between devices: none -> 3.28 us  [the longest x1 2.28 us: shards(): below = lax.ppermute(first, 'band', [(b, a) for a, b in ring])]
    ppermute x0 -> x2, starting transfers between devices: none -> 2.33 us  [the longest x1 2.33 us: shards(): above = lax.ppermute(last, 'band', ring)]
    unnamed x0 -> x4, local copies, waits for them, and re-layouts: none -> 0.6 us
    pallas_call x1 -> x2, Pallas kernels: 15.1 us -> 15.3 us  [the longest x1 13.3 us: shards(): pl.pallas_call(block_kernel, in_specs=[anywhere] * 3 + [hbm] * 6, out_spe...]
  transfers between devices with their start and end apart: 0 -> 2, of which waited for: 0 -> 2; matrix products, arithmetic and copies ran while one was open for 0% -> 0% of each run, Pallas kernels for 0% -> 0%
where the time goes in v2:
time: 44.6 us; the launch traced here: 44.3 us
  blocking collectives  20.8 us (47%)
  Pallas kernels  17.4 us (39%)
  waiting for transfers between devices  3.28 us (7%)
  starting transfers between devices  2.33 us (5%)
  local copies, waits for them, and re-layouts  0.6 us (1%)
    all_to_all x1, blocking collectives, shards(): arrived = lax.all_to_all(payload, 'lon', 0, 0, tiled=True)  20.8 us
    pallas_call x1, Pallas kernels, shards(): pl.pallas_call(block_kernel, in_specs=[anywhere] * 3 + [hbm] * 6, out_spe...  13.3 us
    ppermute x1, starting transfers between devices, shards(): above = lax.ppermute(last, 'band', ring)  2.33 us
    ppermute x1, waiting for transfers between devices, shards(): below = lax.ppermute(first, 'band', [(b, a) for a, b in ring])  2.28 us
    pallas_call x1, Pallas kernels, shards(): pl.pallas_call(mix_kernel, in_specs=[hbm] * 3, out_specs=[vmem] * 3, out_...  2.01 us
    pallas_call x1, Pallas kernels, shards(): pl.pallas_call(pack_kernel, in_specs=[smem, smem, vmem, vmem, vmem], out_...  2.01 us
    ppermute x1, waiting for transfers between devices, shards(): above = lax.ppermute(last, 'band', ring)  1 us
  transfers between devices with their start and end apart: 2, of which 2 were waited for; matrix products, arithmetic and copies ran while one was open for 0% of the time, Pallas kernels for 0%

profile of v2, /device:TPU:1, one launch (start us, length us, event | category | flops | bytes accessed | tf_op | source)
XLA Modules:
  0.0 44.3 jit_solution(12328200146504768135)
XLA Ops:
  0.0 2.0 %pack.1 = (bf16[32,24,128]{2,1,0:T(8,128)(2,1)}, f32[32,256]{1,0:T(8,128)}) custom-call(s32[1,32]{1,0:T(1,128)} %index_ref.1, s32[4]{0:T(128)} %slot_ref.1, bf16[1,1,7680]{2,1,0:T(2,128)(2,1)} %token_ref.1, bf16[4,32,240]{2,1,0:T(8,128)(2,1)} %cache_ref.1, bf16[3,16,16]{2,1,0:T(8,128)(2,1)} %taps_hbm.1), custom_call_target="tpu_custom_call" | custom-call | tf_op jit(solution)/shard_map/pack/pallas_call | solution.py:461
  2.0 20.8 %all_to_all.5.got_hbm = bf16[32,24,128]{2,1,0:T(8,128)(2,1)} all-to-all(bf16[32,24,128]{2,1,0:T(8,128)(2,1)} %get-tuple-element.10), channel_id=1, replica_groups=mesh['lon'=32,'band'=4] {'lon'}, dimensions={0} | all-to-all | bytes 393216 | tf_op jit(solution)/shard_map/all_to_all | solution.py:475
  22.8 2.0 %mix.1 = (bf16[32,512]{1,0:T(8,128)(2,1)}, bf16[8,512]{1,0:T(8,128)(2,1)}, bf16[8,512]{1,0:T(8,128)(2,1)}) custom-call(bf16[32,24,128]{2,1,0:T(8,128)(2,1)} %all_to_all.5.got_hbm, f32[32,256]{1,0:T(8,128)} %get-tuple-element.11.own_hbm, bf16[3,16,16]{2,1,0:T(8,128)(2,1)} %taps_hbm.1), custom_call_target="tpu_custom_call" | custom-call | tf_op jit(solution)/shard_map/mix/pallas_call | solution.py:476
  24.8 2.3 %collective-permute-start = (bf16[8,512]{1,0:T(8,128)(2,1)}, bf16[8,512]{1,0:T(8,128)(2,1)S(1)}, u32[]{:S(2)}, u32[]{:S(2)}) collective-permute-start(bf16[8,512]{1,0:T(8,128)(2,1)} %get-tuple-element.13), channel_id=1, source_target_pairs={{0,1},{1,2},{2,3},{3,0},{4,5},{5,6},{6,7},{7,4},{8,9},{9,10},{10,1... | collective-permute-start | bytes 24584 | tf_op jit(solution)/shard_map/ppermute | solution.py:493
  27.1 0.0 collective-permute-start.1
  27.1 1.0 %collective-permute-done.above_hbm = bf16[8,512]{1,0:T(8,128)(2,1)S(1)} collective-permute-done((bf16[8,512]{1,0:T(8,128)(2,1)}, bf16[8,512]{1,0:T(8,128)(2,1)S(1)}, u32[]{:S(2)}, u32[]{:S(2)}) %collective-permute-start) | collective-permute-done | bytes 8224 | tf_op jit(solution)/shard_map/ppermute | solution.py:493
  28.1 0.0 copy-start
  28.1 2.3 %collective-permute-done.1.below_hbm = bf16[8,512]{1,0:T(8,128)(2,1)S(1)} collective-permute-done((bf16[8,512]{1,0:T(8,128)(2,1)}, bf16[8,512]{1,0:T(8,128)(2,1)S(1)}, u32[]{:S(2)}, u32[]{:S(2)}) %collective-permute-start.1) | collective-permute-done | bytes 8224 | tf_op jit(solution)/shard_map/ppermute | solution.py:494
  30.4 0.0 copy-start.1
  30.4 0.0 copy-done
  30.4 0.6 %copy-done.1 = bf16[8,512]{1,0:T(8,128)(2,1)} copy-done((bf16[8,512]{1,0:T(8,128)(2,1)}, bf16[8,512]{1,0:T(8,128)(2,1)S(1)}, u32[]{:S(2)}) %copy-start.1) | copy-done | bytes 8216
  31.0 13.3 %block.1 = bf16[30,64,256]{2,1,0:T(8,128)(2,1)} custom-call(bf16[32,512]{1,0:T(8,128)(2,1)} %get-tuple-element.12.temporal_hbm, bf16[8,512]{1,0:T(8,128)(2,1)} %copy-done, bf16[8,512]{1,0:T(8,128)(2,1)} %copy-done.1, f32[2,256]{1,0:T(2,128)} %low_gain_hbm.1, f32[2,256]{1,0:T(2,128)} %high_gain_hbm.1, bf16[3,48,256]{2,1,0:T(8,128)(2,1)} %bitcast.6, ...), custom_call_target="tpu_custom_call" | custom-call | tf_op jit(solution)/shard_map/block/pallas_call | solution.py:495
Async XLA Ops:
  24.8 3.3 %collective-permute-start = (bf16[8,512]{1,0:T(8,128)(2,1)}, bf16[8,512]{1,0:T(8,128)(2,1)S(1)}, u32[]{:S(2)}, u32[]{:S(2)}) collective-permute-start(bf16[8,512]{1,0:T(8,128)(2,1)} %get-tuple-element.13), channel_id=1, source_target_pairs={{0,1},{1,2},{2,3},{3,0},{4,5},{5,6},{6,7},{7,4},{8,9},{9,10},{10,1... | collective-permute-start | bytes 24584 | tf_op jit(solution)/shard_map/ppermute | solution.py:493
  27.1 3.3 %collective-permute-start.1 = (bf16[8,512]{1,0:T(8,128)(2,1)}, bf16[8,512]{1,0:T(8,128)(2,1)S(1)}, u32[]{:S(2)}, u32[]{:S(2)}) collective-permute-start(bf16[8,512]{1,0:T(8,128)(2,1)} %get-tuple-element.14), channel_id=1, source_target_pairs={{1,0},{2,1},{3,2},{0,3},{5,4},{6,5},{7,6},{4,7},{9,8},{10,9},{11,1... | collective-permute-start | bytes 24584 | tf_op jit(solution)/shard_map/ppermute | solution.py:494
  28.1 2.3 %copy-start = (bf16[8,512]{1,0:T(8,128)(2,1)}, bf16[8,512]{1,0:T(8,128)(2,1)S(1)}, u32[]{:S(2)}) copy-start(bf16[8,512]{1,0:T(8,128)(2,1)S(1)} %collective-permute-done.above_hbm) | copy-start | bytes 24580
  30.4 0.6 %copy-start.1 = (bf16[8,512]{1,0:T(8,128)(2,1)}, bf16[8,512]{1,0:T(8,128)(2,1)S(1)}, u32[]{:S(2)}) copy-start(bf16[8,512]{1,0:T(8,128)(2,1)S(1)} %collective-permute-done.1.below_hbm) | copy-start | bytes 24580

commit v3 on v2

--- a/solution.py
+++ b/solution.py
@@ -178,8 +178,9 @@
     w_in,
     w_low,
     w_up,
+    w_phase,
     w_high,
-    w_phase,
+    w_mid,
     u_ref,
     open_ref,
     a1_ref,
@@ -199,10 +200,13 @@
     copies.append(pltpu.make_async_copy(w_low_hbm.at[0], w_low.at[0], in_sem.at[3]))
     copies.append(pltpu.make_async_copy(w_low_hbm.at[1], w_low.at[1], in_sem.at[4]))
     copies.append(pltpu.make_async_copy(w_up_hbm, w_up, in_sem.at[5]))
-    copies.append(pltpu.make_async_copy(w_high_hbm.at[0], w_high.at[0], in_sem.at[6]))
-    copies.append(pltpu.make_async_copy(w_high_hbm.at[1], w_high.at[1], in_sem.at[7]))
+    for n in range(2):
+        for k in range(3):
+            target = w_mid.at[n] if k == 1 else w_high.at[n, k // 2 * 3]
+            pair = (w_high_hbm.at[n, :, k], target)
+            copies.append(pltpu.make_async_copy(*pair, in_sem.at[6 + 3 * n + k]))
     small = [
-        pltpu.make_async_copy(source, target, in_sem.at[8 + n])
+        pltpu.make_async_copy(source, target, in_sem.at[12 + n])
         for n, (source, target) in enumerate(
             (
                 (temporal_hbm, temporal_ref),
@@ -331,6 +335,40 @@
                         total = one if total is None else total + one
                 at = (2 * r + c) * CH
                 w_phase[a, odd, at : at + CH, :] = total.astype(BF16)
+
+    def sum_weights(n, p):
+        outer = w_high[n, 0, p].astype(F32) + w_high[n, 3, p].astype(F32)
+        inner = w_mid[n, p].astype(F32)
+        w_high[n, 1, p] = (0.5 * (outer + inner)).astype(BF16)
+        w_high[n, 2, p] = (0.5 * (outer - inner)).astype(BF16)
+
+    beside = {}
+    for k in range(4):
+        beside[3 + k] = (copies[5:6] if k == 0 else (), phase_weights, (k // 2, k % 2))
+    for p in range(3):
+        beside[7 + p] = (copies[6:9] if p == 0 else (), sum_weights, (0, p))
+        beside[17 + p] = (copies[9:12] if p == 0 else (), sum_weights, (1, p))
+
+    held = []
+
+    def quads(evens, odd, odd_next):
+        even_last, even = evens
+        parts = (even_last - even, odd + even, even - odd, odd - odd_next)
+        return [part.astype(BF16) for part in parts]
+
+    def pairs(ref, row, count, weight):
+        m = []
+        for k in range(4):
+            total = None
+            for p in range(3):
+                part = jnp.dot(
+                    ref[(row + p) * HIGH : (row + p + count) * HIGH, CH * k : CH * k + CH],
+                    weight[k, p],
+                    preferred_element_type=F32,
+                )
+                total = part if total is None else total + part
+            m.append(total)
+        return m[0] + m[1] + m[2], m[1] - m[2] - m[3]
 
     for n in (0, 17):
         for a in range(2):
@@ -371,57 +409,58 @@
                     turned = jnp.concatenate(
                         [mix_ref[odd, half, 0 : 17 * HIGH, :] for half in range(2)], axis=1
                     )
-                    act = outside(act, HIGH, n, 1, 1, 34).astype(BF16)
-                    turned = outside(turned, HIGH, n, 1, 1, 34).astype(BF16)
-                    slot, beside = (1, 3) if odd else (2, 0)
+                    act = outside(act, HIGH, n, 1, 1, 34)
+                    turned = outside(turned, HIGH, n, 1, 1, 34)
+                    if odd:
+                        parts = quads(held.pop(), act, turned)
+                    else:
+                        held.append((turned, act))
                     for i in range(17):
                         rows = slice(i * HIGH, (i + 1) * HIGH)
                         at = (2 * (n + i) + a) * HIGH
-                        s1_ref[at : at + HIGH, CH * slot : CH * slot + CH] = act[rows]
-                        s1_ref[at : at + HIGH, CH * beside : CH * beside + CH] = turned[rows]
+                        if odd:
+                            for k in range(4):
+                                s1_ref[at : at + HIGH, CH * k : CH * k + CH] = parts[k][rows]
                         raw_ref[at : at + HIGH, CH * odd : CH * odd + CH] = value[rows]
 
                 task(product, finish)
 
     for row, count in cuts(66, 6):
-        for odd in range(2):
-
-            def product(row=row, count=count, odd=odd):
-                return conv(s1_ref, HIGH, row, count, 0 if odd else CH, w_high.at[0])
-
-            def finish(value, row=row, count=count, odd=odd):
-                act = activate(value, high_gain_ref[1:2, :])
-                act = outside(act, HIGH, row, 1, 1, 66)
-                slot, beside = (1, 3) if odd else (2, 0)
-                rows = slice(row * HIGH, (row + count) * HIGH)
-                s2_ref[rows, CH * slot : CH * slot + CH] = act.astype(BF16)
-                s2_ref[rows, CH * beside : CH * beside + CH] = roll_rows(
-                    act, -1 if odd else 1
-                ).astype(BF16)
-
-            task(product, finish, copies[6:7] if row == 0 and odd == 0 else None)
+
+        def product(row=row, count=count):
+            return pairs(s1_ref, row, count, w_high.at[0])
+
+        def finish(values, row=row, count=count):
+            odd, even = (
+                outside(activate(value, high_gain_ref[1:2, :]), HIGH, row, 1, 1, 66)
+                for value in values
+            )
+            parts = quads((roll_rows(even, 1), even), odd, roll_rows(odd, -1))
+            for k in range(4):
+                s2_ref[row * HIGH : (row + count) * HIGH, CH * k : CH * k + CH] = parts[k]
+
+        task(product, finish)
 
     outs = []
     for n, row in enumerate(range(0, 64, 16)):
-        for odd in range(2):
-
-            def product(row=row, odd=odd):
-                return conv(s2_ref, HIGH, row, 16, 0 if odd else CH, w_high.at[1])
-
-            def finish(value, n=n, row=row, odd=odd):
-                rows = slice((row + 2) * HIGH, (row + 18) * HIGH)
-                value = value + raw_ref[rows, odd * CH : odd * CH + CH].astype(F32)
+
+        def product(row=row):
+            return pairs(s2_ref, row, 16, w_high.at[1])
+
+        def finish(values, n=n, row=row):
+            rows = slice((row + 2) * HIGH, (row + 18) * HIGH)
+            for odd in range(2):
+                value = values[1 - odd] + raw_ref[rows, odd * CH : odd * CH + CH].astype(F32)
                 value = jnp.swapaxes(value.reshape(16, HIGH, CH), 0, 1).astype(BF16)
                 for j in range(COLS):
                     out_ref[2 * j + odd, row : row + 16, :] = value[j + odd]
-                if odd:
-                    copy = pltpu.make_async_copy(
-                        out_ref.at[:, row : row + 16], out_hbm.at[:, row : row + 16], out_sem.at[n]
-                    )
-                    copy.start()
-                    outs.append(copy)
-
-            task(product, finish, copies[7:8] if row == 0 and odd == 0 else None)
+            copy = pltpu.make_async_copy(
+                out_ref.at[:, row : row + 16], out_hbm.at[:, row : row + 16], out_sem.at[n]
+            )
+            copy.start()
+            outs.append(copy)
+
+        task(product, finish)
 
     before = None
     for number, (product, finish, wait) in enumerate(tasks):
@@ -431,10 +470,11 @@
         if before is not None:
             before[0](before[1])
         before = (finish, value)
-        if number == 4:
-            copies[5].wait()
-        if 4 <= number <= 7:
-            phase_weights((number - 4) // 2, (number - 4) % 2)
+        if number in beside:
+            arrive, work, which = beside[number]
+            for copy in arrive:
+                copy.wait()
+            work(*which)
     before[0](before[1])
     for copy in outs:
         copy.wait()
@@ -505,8 +545,9 @@
             pltpu.VMEM((3, 128, CH), BF16),
             pltpu.VMEM((2, 3, 3 * CH, CH), BF16),
             pltpu.VMEM((9, CH, CH), BF16),
-            pltpu.VMEM((2, 3, 3 * CH, CH), BF16),
             pltpu.VMEM((2, 2, 4 * CH, CH), BF16),
+            pltpu.VMEM((2, 4, 3, CH, CH), BF16),
+            pltpu.VMEM((2, 3, CH, CH), BF16),
             pltpu.VMEM((48 * LOW, 128), F32),
             pltpu.VMEM((40 * LOW, CH), F32),
             pltpu.VMEM((40 * LOW, 3 * CH), BF16),
@@ -518,7 +559,7 @@
             pltpu.VMEM((66 * HIGH, 4 * CH), BF16),
             pltpu.VMEM((2, 2, 24 * HIGH, 128), F32),
             pltpu.VMEM((2 * COLS, 2 * ROWS, CH), BF16),
-            pltpu.SemaphoreType.DMA((13,)),
+            pltpu.SemaphoreType.DMA((17,)),
             pltpu.SemaphoreType.DMA((4,)),
         ],
         compiler_params=pltpu.CompilerParams(vmem_limit_bytes=56 * 1024 * 1024),
@@ -532,7 +573,7 @@
         input_weight.reshape(3, 48, CH),
         latent_conv_weights.reshape(2, 3, 3 * CH, CH),
         upsampled_weight,
-        upper_conv_weights.reshape(2, 3, 3 * CH, CH),
+        upper_conv_weights.reshape(2, 3, 3, CH, CH),
     )
     return decoded.transpose(1, 0, 2)
 

time: 44.6 us -> 43.9 us (0.984)
  Pallas kernels: 17.4 us -> 16.6 us
    pallas_call x1, Pallas kernels: 13.3 us -> 12.6 us  [shards(): pl.pallas_call(block_kernel, in_specs=[anywhere] * 3 + [hbm] * 6, out_spe...]
where the time goes in v3:
time: 43.9 us; the launch traced here: 43.6 us
  blocking collectives  20.8 us (47%)
  Pallas kernels  16.6 us (38%)
  waiting for transfers between devices  3.28 us (7%)
  starting transfers between devices  2.33 us (5%)
  local copies, waits for them, and re-layouts  0.6 us (1%)
    all_to_all x1, blocking collectives, shards(): arrived = lax.all_to_all(payload, 'lon', 0, 0, tiled=True)  20.8 us
    pallas_call x1, Pallas kernels, shards(): pl.pallas_call(block_kernel, in_specs=[anywhere] * 3 + [hbm] * 6, out_spe...  12.6 us
    ppermute x1, starting transfers between devices, shards(): above = lax.ppermute(last, 'band', ring)  2.33 us
    ppermute x1, waiting for transfers between devices, shards(): below = lax.ppermute(first, 'band', [(b, a) for a, b in ring])  2.28 us
    pallas_call x1, Pallas kernels, shards(): pl.pallas_call(mix_kernel, in_specs=[hbm] * 3, out_specs=[vmem] * 3, out_...  2.01 us
    pallas_call x1, Pallas kernels, shards(): pl.pallas_call(pack_kernel, in_specs=[smem, smem, vmem, vmem, vmem], out_...  2.01 us
    ppermute x1, waiting for transfers between devices, shards(): above = lax.ppermute(last, 'band', ring)  1 us
  transfers between devices with their start and end apart: 2, of which 2 were waited for; matrix products, arithmetic and copies ran while one was open for 0% of the time, Pallas kernels for 0%

profile of v3, /device:TPU:1, one launch (start us, length us, event | category | flops | bytes accessed | tf_op | source)
XLA Modules:
  0.0 43.6 jit_solution(5303330691407637969)
XLA Ops:
  0.0 2.0 %pack.1 = (bf16[32,24,128]{2,1,0:T(8,128)(2,1)}, f32[32,256]{1,0:T(8,128)}) custom-call(s32[1,32]{1,0:T(1,128)} %index_ref.1, s32[4]{0:T(128)} %slot_ref.1, bf16[1,1,7680]{2,1,0:T(2,128)(2,1)} %token_ref.1, bf16[4,32,240]{2,1,0:T(8,128)(2,1)} %cache_ref.1, bf16[3,16,16]{2,1,0:T(8,128)(2,1)} %taps_hbm.1), custom_call_target="tpu_custom_call" | custom-call | tf_op jit(solution)/shard_map/pack/pallas_call | solution.py:501
  2.0 20.8 %all_to_all.5.got_hbm = bf16[32,24,128]{2,1,0:T(8,128)(2,1)} all-to-all(bf16[32,24,128]{2,1,0:T(8,128)(2,1)} %get-tuple-element.10), channel_id=1, replica_groups=mesh['lon'=32,'band'=4] {'lon'}, dimensions={0} | all-to-all | bytes 393216 | tf_op jit(solution)/shard_map/all_to_all | solution.py:515
  22.8 2.0 %mix.1 = (bf16[32,512]{1,0:T(8,128)(2,1)}, bf16[8,512]{1,0:T(8,128)(2,1)}, bf16[8,512]{1,0:T(8,128)(2,1)}) custom-call(bf16[32,24,128]{2,1,0:T(8,128)(2,1)} %all_to_all.5.got_hbm, f32[32,256]{1,0:T(8,128)} %get-tuple-element.11.own_hbm, bf16[3,16,16]{2,1,0:T(8,128)(2,1)} %taps_hbm.1), custom_call_target="tpu_custom_call" | custom-call | tf_op jit(solution)/shard_map/mix/pallas_call | solution.py:516
  24.8 2.3 %collective-permute-start = (bf16[8,512]{1,0:T(8,128)(2,1)}, bf16[8,512]{1,0:T(8,128)(2,1)S(1)}, u32[]{:S(2)}, u32[]{:S(2)}) collective-permute-start(bf16[8,512]{1,0:T(8,128)(2,1)} %get-tuple-element.13), channel_id=1, source_target_pairs={{0,1},{1,2},{2,3},{3,0},{4,5},{5,6},{6,7},{7,4},{8,9},{9,10},{10,1... | collective-permute-start | bytes 24584 | tf_op jit(solution)/shard_map/ppermute | solution.py:533
  27.1 0.0 collective-permute-start.1
  27.1 1.0 %collective-permute-done.above_hbm = bf16[8,512]{1,0:T(8,128)(2,1)S(1)} collective-permute-done((bf16[8,512]{1,0:T(8,128)(2,1)}, bf16[8,512]{1,0:T(8,128)(2,1)S(1)}, u32[]{:S(2)}, u32[]{:S(2)}) %collective-permute-start) | collective-permute-done | bytes 8224 | tf_op jit(solution)/shard_map/ppermute | solution.py:533
  28.1 0.0 copy-start
  28.1 2.3 %collective-permute-done.1.below_hbm = bf16[8,512]{1,0:T(8,128)(2,1)S(1)} collective-permute-done((bf16[8,512]{1,0:T(8,128)(2,1)}, bf16[8,512]{1,0:T(8,128)(2,1)S(1)}, u32[]{:S(2)}, u32[]{:S(2)}) %collective-permute-start.1) | collective-permute-done | bytes 8224 | tf_op jit(solution)/shard_map/ppermute | solution.py:534
  30.4 0.0 copy-start.1
  30.4 0.0 copy-done
  30.4 0.6 %copy-done.1 = bf16[8,512]{1,0:T(8,128)(2,1)} copy-done((bf16[8,512]{1,0:T(8,128)(2,1)}, bf16[8,512]{1,0:T(8,128)(2,1)S(1)}, u32[]{:S(2)}) %copy-start.1) | copy-done | bytes 8216
  31.0 12.6 %block.1 = bf16[30,64,256]{2,1,0:T(8,128)(2,1)} custom-call(bf16[32,512]{1,0:T(8,128)(2,1)} %get-tuple-element.12.temporal_hbm, bf16[8,512]{1,0:T(8,128)(2,1)} %copy-done, bf16[8,512]{1,0:T(8,128)(2,1)} %copy-done.1, f32[2,256]{1,0:T(2,128)} %low_gain_hbm.1, f32[2,256]{1,0:T(2,128)} %high_gain_hbm.1, bf16[3,48,256]{2,1,0:T(8,128)(2,1)} %bitcast.6, ...), custom_call_target="tpu_custom_call" | custom-call | tf_op jit(solution)/shard_map/block/pallas_call | solution.py:535
Async XLA Ops:
  24.8 3.3 %collective-permute-start = (bf16[8,512]{1,0:T(8,128)(2,1)}, bf16[8,512]{1,0:T(8,128)(2,1)S(1)}, u32[]{:S(2)}, u32[]{:S(2)}) collective-permute-start(bf16[8,512]{1,0:T(8,128)(2,1)} %get-tuple-element.13), channel_id=1, source_target_pairs={{0,1},{1,2},{2,3},{3,0},{4,5},{5,6},{6,7},{7,4},{8,9},{9,10},{10,1... | collective-permute-start | bytes 24584 | tf_op jit(solution)/shard_map/ppermute | solution.py:533
  27.1 3.3 %collective-permute-start.1 = (bf16[8,512]{1,0:T(8,128)(2,1)}, bf16[8,512]{1,0:T(8,128)(2,1)S(1)}, u32[]{:S(2)}, u32[]{:S(2)}) collective-permute-start(bf16[8,512]{1,0:T(8,128)(2,1)} %get-tuple-element.14), channel_id=1, source_target_pairs={{1,0},{2,1},{3,2},{0,3},{5,4},{6,5},{7,6},{4,7},{9,8},{10,9},{11,1... | collective-permute-start | bytes 24584 | tf_op jit(solution)/shard_map/ppermute | solution.py:534
  28.1 2.3 %copy-start = (bf16[8,512]{1,0:T(8,128)(2,1)}, bf16[8,512]{1,0:T(8,128)(2,1)S(1)}, u32[]{:S(2)}) copy-start(bf16[8,512]{1,0:T(8,128)(2,1)S(1)} %collective-permute-done.above_hbm) | copy-start | bytes 24580
  30.4 0.6 %copy-start.1 = (bf16[8,512]{1,0:T(8,128)(2,1)}, bf16[8,512]{1,0:T(8,128)(2,1)S(1)}, u32[]{:S(2)}) copy-start(bf16[8,512]{1,0:T(8,128)(2,1)S(1)} %collective-permute-done.1.below_hbm) | copy-start | bytes 24580

commit v4 on v3

--- a/solution.py
+++ b/solution.py
@@ -37,10 +37,8 @@
 
 
 def block_diagonal(tap):
-    rows = jnp.where(iota((128, LAT), 0) % LAT == iota((128, LAT), 1), 1.0, 0.0).astype(BF16)
-    cols = jnp.where(iota((LAT, 128), 1) % LAT == iota((LAT, 128), 0), 1.0, 0.0).astype(BF16)
-    tall = jnp.dot(rows, tap, preferred_element_type=F32).astype(BF16)
-    full = jnp.dot(tall, cols, preferred_element_type=F32)
+    wide = jnp.concatenate([tap.astype(F32)] * (128 // LAT), axis=1)
+    full = jnp.concatenate([wide] * (128 // LAT), axis=0)
     same = iota((128, 128), 0) // LAT == iota((128, 128), 1) // LAT
     return jnp.where(same, full, 0.0).astype(BF16)
 

time: 43.9 us -> 43.7 us (level)
  no operation moved by 1% of the time
where the time goes in v4:
time: 43.7 us; the launch traced here: 43.4 us
  blocking collectives  20.8 us (48%)
  Pallas kernels  16.4 us (38%)
  waiting for transfers between devices  3.28 us (8%)
  starting transfers between devices  2.33 us (5%)
  local copies, waits for them, and re-layouts  0.6 us (1%)
    all_to_all x1, blocking collectives, shards(): arrived = lax.all_to_all(payload, 'lon', 0, 0, tiled=True)  20.8 us
    pallas_call x1, Pallas kernels, shards(): pl.pallas_call(block_kernel, in_specs=[anywhere] * 3 + [hbm] * 6, out_spe...  12.6 us
    ppermute x1, starting transfers between devices, shards(): above = lax.ppermute(last, 'band', ring)  2.33 us
    ppermute x1, waiting for transfers between devices, shards(): below = lax.ppermute(first, 'band', [(b, a) for a, b in ring])  2.28 us
    pallas_call x1, Pallas kernels, shards(): pl.pallas_call(mix_kernel, in_specs=[hbm] * 3, out_specs=[vmem] * 3, out_...  1.97 us
    pallas_call x1, Pallas kernels, shards(): pl.pallas_call(pack_kernel, in_specs=[smem, smem, vmem, vmem, vmem], out_...  1.83 us
    ppermute x1, waiting for transfers between devices, shards(): above = lax.ppermute(last, 'band', ring)  1 us
  transfers between devices with their start and end apart: 2, of which 2 were waited for; matrix products, arithmetic and copies ran while one was open for 0% of the time, Pallas kernels for 0%

profile of v4, /device:TPU:1, one launch (start us, length us, event | category | flops | bytes accessed | tf_op | source)
XLA Modules:
  0.0 43.4 jit_solution(18354719703624229200)
XLA Ops:
  0.0 1.8 %pack.1 = (bf16[32,24,128]{2,1,0:T(8,128)(2,1)}, f32[32,256]{1,0:T(8,128)}) custom-call(s32[1,32]{1,0:T(1,128)} %index_ref.1, s32[4]{0:T(128)} %slot_ref.1, bf16[1,1,7680]{2,1,0:T(2,128)(2,1)} %token_ref.1, bf16[4,32,240]{2,1,0:T(8,128)(2,1)} %cache_ref.1, bf16[3,16,16]{2,1,0:T(8,128)(2,1)} %taps_hbm.1), custom_call_target="tpu_custom_call" | custom-call | tf_op jit(solution)/shard_map/pack/pallas_call | solution.py:499
  1.8 20.8 %all_to_all.5.got_hbm = bf16[32,24,128]{2,1,0:T(8,128)(2,1)} all-to-all(bf16[32,24,128]{2,1,0:T(8,128)(2,1)} %get-tuple-element.10), channel_id=1, replica_groups=mesh['lon'=32,'band'=4] {'lon'}, dimensions={0} | all-to-all | bytes 393216 | tf_op jit(solution)/shard_map/all_to_all | solution.py:513
  22.6 2.0 %mix.1 = (bf16[32,512]{1,0:T(8,128)(2,1)}, bf16[8,512]{1,0:T(8,128)(2,1)}, bf16[8,512]{1,0:T(8,128)(2,1)}) custom-call(bf16[32,24,128]{2,1,0:T(8,128)(2,1)} %all_to_all.5.got_hbm, f32[32,256]{1,0:T(8,128)} %get-tuple-element.11.own_hbm, bf16[3,16,16]{2,1,0:T(8,128)(2,1)} %taps_hbm.1), custom_call_target="tpu_custom_call" | custom-call | tf_op jit(solution)/shard_map/mix/pallas_call | solution.py:514
  24.6 2.3 %collective-permute-start = (bf16[8,512]{1,0:T(8,128)(2,1)}, bf16[8,512]{1,0:T(8,128)(2,1)S(1)}, u32[]{:S(2)}, u32[]{:S(2)}) collective-permute-start(bf16[8,512]{1,0:T(8,128)(2,1)} %get-tuple-element.13), channel_id=1, source_target_pairs={{0,1},{1,2},{2,3},{3,0},{4,5},{5,6},{6,7},{7,4},{8,9},{9,10},{10,1... | collective-permute-start | bytes 24584 | tf_op jit(solution)/shard_map/ppermute | solution.py:531
  26.9 0.0 collective-permute-start.1
  26.9 1.0 %collective-permute-done.above_hbm = bf16[8,512]{1,0:T(8,128)(2,1)S(1)} collective-permute-done((bf16[8,512]{1,0:T(8,128)(2,1)}, bf16[8,512]{1,0:T(8,128)(2,1)S(1)}, u32[]{:S(2)}, u32[]{:S(2)}) %collective-permute-start) | collective-permute-done | bytes 8224 | tf_op jit(solution)/shard_map/ppermute | solution.py:531
  27.9 0.0 copy-start
  27.9 2.3 %collective-permute-done.1.below_hbm = bf16[8,512]{1,0:T(8,128)(2,1)S(1)} collective-permute-done((bf16[8,512]{1,0:T(8,128)(2,1)}, bf16[8,512]{1,0:T(8,128)(2,1)S(1)}, u32[]{:S(2)}, u32[]{:S(2)}) %collective-permute-start.1) | collective-permute-done | bytes 8224 | tf_op jit(solution)/shard_map/ppermute | solution.py:532
  30.2 0.0 copy-start.1
  30.2 0.0 copy-done
  30.2 0.6 %copy-done.1 = bf16[8,512]{1,0:T(8,128)(2,1)} copy-done((bf16[8,512]{1,0:T(8,128)(2,1)}, bf16[8,512]{1,0:T(8,128)(2,1)S(1)}, u32[]{:S(2)}) %copy-start.1) | copy-done | bytes 8216
  30.8 12.6 %block.1 = bf16[30,64,256]{2,1,0:T(8,128)(2,1)} custom-call(bf16[32,512]{1,0:T(8,128)(2,1)} %get-tuple-element.12.temporal_hbm, bf16[8,512]{1,0:T(8,128)(2,1)} %copy-done, bf16[8,512]{1,0:T(8,128)(2,1)} %copy-done.1, f32[2,256]{1,0:T(2,128)} %low_gain_hbm.1, f32[2,256]{1,0:T(2,128)} %high_gain_hbm.1, bf16[3,48,256]{2,1,0:T(8,128)(2,1)} %bitcast.6, ...), custom_call_target="tpu_custom_call" | custom-call | tf_op jit(solution)/shard_map/block/pallas_call | solution.py:533
Async XLA Ops:
  24.6 3.3 %collective-permute-start = (bf16[8,512]{1,0:T(8,128)(2,1)}, bf16[8,512]{1,0:T(8,128)(2,1)S(1)}, u32[]{:S(2)}, u32[]{:S(2)}) collective-permute-start(bf16[8,512]{1,0:T(8,128)(2,1)} %get-tuple-element.13), channel_id=1, source_target_pairs={{0,1},{1,2},{2,3},{3,0},{4,5},{5,6},{6,7},{7,4},{8,9},{9,10},{10,1... | collective-permute-start | bytes 24584 | tf_op jit(solution)/shard_map/ppermute | solution.py:531
  26.9 3.3 %collective-permute-start.1 = (bf16[8,512]{1,0:T(8,128)(2,1)}, bf16[8,512]{1,0:T(8,128)(2,1)S(1)}, u32[]{:S(2)}, u32[]{:S(2)}) collective-permute-start(bf16[8,512]{1,0:T(8,128)(2,1)} %get-tuple-element.14), channel_id=1, source_target_pairs={{1,0},{2,1},{3,2},{0,3},{5,4},{6,5},{7,6},{4,7},{9,8},{10,9},{11,1... | collective-permute-start | bytes 24584 | tf_op jit(solution)/shard_map/ppermute | solution.py:532
  27.9 2.3 %copy-start = (bf16[8,512]{1,0:T(8,128)(2,1)}, bf16[8,512]{1,0:T(8,128)(2,1)S(1)}, u32[]{:S(2)}) copy-start(bf16[8,512]{1,0:T(8,128)(2,1)S(1)} %collective-permute-done.above_hbm) | copy-start | bytes 24580
  30.2 0.6 %copy-start.1 = (bf16[8,512]{1,0:T(8,128)(2,1)}, bf16[8,512]{1,0:T(8,128)(2,1)S(1)}, u32[]{:S(2)}) copy-start(bf16[8,512]{1,0:T(8,128)(2,1)S(1)} %collective-permute-done.1.below_hbm) | copy-start | bytes 24580
